TPU v7x, 128 devices: a whole 4x4x4 slice. The times are simulated.
128 devices in a mesh: bins: 16 (over y, z), chan: 8 (over x, core).
Axes of the slice: x: 4, y: 4, z: 4, core: 2. Of those that a mesh axis runs over, the one named last changes fastest.
Arguments:
- tokens_in: bfloat16 [8192, 2048], P('bins', 'chan'), may hold values from -6 to 6
- filters: bfloat16 [8192, 2048], P('bins', 'chan'), may hold values from -0.0625 to 0.0625
- gate: bfloat16 [8192, 2048], P('bins', 'chan'), may hold values from -6 to 6
- skip: float32 [2048], P('chan'), may hold values from 0.5 to 1.5
- out_grad: bfloat16 [8192, 4096], P('bins', 'chan'), may hold values from -6 to 6
- out_weight: bfloat16 [2048, 4096], P('chan'), may hold values from -0.09375 to 0.09375
- owner: int32 [16, 512], P(None, 'bins'), may hold values from 0 to 15, as said below
- slot: int32 [16, 512], P(None, 'bins'), may hold values from 0 to 1023, as said below
Outputs:
- gate_grad: bfloat16 [16, 512, 2048], P(None, 'bins', 'chan')
- filter_grad: float32 [16, 512, 2048], P(None, 'bins', 'chan')
- grad_rows: bfloat16 [16384, 2048], P('bins', 'chan')
Inputs may be any that keep to these rules, and one draw needn't show every extreme that they name: Let the column group j be the entries [i, r] with j * 32 <= r < (j + 1) * 32, all i. Within one column group at most 64 entries name the same owner, and in every draw some owner is named exactly 64 times by every column group. An entry of column group j (as for owner) lies in j * 64 to (j + 1) * 64 - 1; no two tokens share an owner and a slot; in every draw some owner has all 1024 slots used.
All inputs are finite; a program needn't handle non-finite values.
Results may differ from a plain program's by a relative error of at most 0.012.
Values may be sent and summed in bfloat16 or wider, within the bound.
A program may use at most 128 MiB of HBM per device.

v0:
```python
import math

import jax
import jax.numpy as jnp
from jax import lax
from jax.sharding import PartitionSpec as P

exact_mode = lax.Precision.HIGHEST


def angles(index, period):
    return 2.0 * math.pi / period * (index % period).astype(jnp.float32)


def contract(table, values, form):
    return jnp.einsum(form, table, values, precision=exact_mode)


def product(left_re, left_im, right_re, right_im):
    return (left_re * right_re - left_im * right_im, left_re * right_im + left_im * right_re)


def shards(tokens_in, filters, gate, skip, out_grad, out_weight, owner, slot):
    blocks = lax.axis_size("bins")
    my_index = lax.axis_index("bins")
    tok_rows, channels = tokens_in.shape
    col_rows = tok_rows // blocks
    length = 2 * blocks * tok_rows
    block_ids = jnp.arange(blocks, dtype=jnp.int32)
    bin_order = jnp.stack(
        [block_ids, jnp.where(block_ids == 0, blocks, 2 * blocks - block_ids)], axis=1
    ).reshape(2 * blocks)
    block_angle = angles(bin_order[:, None] * block_ids[None, :], 2 * blocks)
    block_cos = jnp.cos(block_angle)
    block_sin = jnp.sin(block_angle)
    back_cos = block_cos.T
    back_sin = block_sin.T
    column_ids = my_index * col_rows + jnp.arange(col_rows, dtype=jnp.int32)
    ahead_angle = angles(bin_order[:, None] * column_ids[None, :], length)[:, :, None]
    ahead_cos = jnp.cos(ahead_angle)
    ahead_sin = jnp.sin(ahead_angle)
    own_bins = lax.dynamic_slice_in_dim(bin_order, 2 * my_index, 2)
    positions = jnp.arange(tok_rows, dtype=jnp.int32)
    return_angle = angles(own_bins[:, None] * positions[None, :], length)[:, :, None]
    return_cos = jnp.cos(return_angle)
    return_sin = jnp.sin(return_angle)
    inner_angle = angles(positions[:, None] * positions[None, :], tok_rows)
    inner_cos = jnp.cos(inner_angle)
    inner_sin = jnp.sin(inner_angle)
    upstream = lax.dot_general(
        lax.all_gather(out_grad, "chan", axis=1, tiled=True),
        out_weight,
        (((1,), (1,)), ((), ())),
        preferred_element_type=jnp.float32,
    )
    g_rounded = upstream.astype(jnp.bfloat16)
    grad_in = (g_rounded.astype(jnp.float32) * gate.astype(jnp.float32)).astype(jnp.bfloat16)
    grid_shape = (blocks, col_rows, channels)
    tok_cols, filt_cols, grad_cols, gout_cols = (
        lax.all_to_all(
            tokens_in.reshape(grid_shape), "bins", split_axis=0, concat_axis=0, tiled=True
        ),
        lax.all_to_all(
            filters.reshape(grid_shape), "bins", split_axis=0, concat_axis=0, tiled=True
        ),
        lax.all_to_all(
            grad_in.reshape(grid_shape), "bins", split_axis=0, concat_axis=0, tiled=True
        ),
        lax.all_to_all(
            g_rounded.reshape(grid_shape), "bins", split_axis=0, concat_axis=0, tiled=True
        ),
    )
    tok_real = tok_cols.astype(jnp.float32)
    filt_real = filt_cols.astype(jnp.float32)
    grad_real = grad_cols.astype(jnp.float32)
    real_stack = jnp.stack([tok_real, filt_real, grad_real])
    part_re = contract(block_cos, real_stack, "ki,sirc->skrc")
    part_im = -contract(block_sin, real_stack, "ki,sirc->skrc")
    turned = jnp.stack(
        [part_re * ahead_cos + part_im * ahead_sin, part_im * ahead_cos - part_re * ahead_sin],
        axis=1,
    )
    arrived = lax.all_to_all(turned, "bins", split_axis=2, concat_axis=3, tiled=True)
    came_re = arrived[:, 0]
    came_im = arrived[:, 1]
    spec_re = contract(inner_cos, came_re, "kr,slrc->slkc") + contract(
        inner_sin, came_im, "kr,slrc->slkc"
    )
    spec_im = contract(inner_cos, came_im, "kr,slrc->slkc") - contract(
        inner_sin, came_re, "kr,slrc->slkc"
    )
    spec_re, spec_im = (spec_re, spec_im)
    x_re, x_im = (spec_re[0], spec_im[0])
    h_re, h_im = (spec_re[1], spec_im[1])
    y_re, y_im = (spec_re[2], spec_im[2])
    conv_re, conv_im = product(x_re, x_im, h_re, h_im)
    back_re, back_im = product(h_re, -h_im, y_re, y_im)
    lag_re, lag_im = product(y_re, y_im, x_re, -x_im)
    freq_re = jnp.stack([conv_re, back_re, lag_re])
    freq_im = jnp.stack([conv_im, back_im, lag_im])
    sum_re = contract(inner_cos, freq_re, "rk,slkc->slrc") - contract(
        inner_sin, freq_im, "rk,slkc->slrc"
    )
    sum_im = contract(inner_cos, freq_im, "rk,slkc->slrc") + contract(
        inner_sin, freq_re, "rk,slkc->slrc"
    )
    twist_re = sum_re * return_cos - sum_im * return_sin
    twist_im = sum_re * return_sin + sum_im * return_cos
    turned = jnp.stack([twist_re, twist_im], axis=1)
    arrived = lax.all_to_all(turned, "bins", split_axis=3, concat_axis=2, tiled=True)
    came_re = arrived[:, 0]
    came_im = arrived[:, 1]
    out_re = contract(back_cos, came_re, "ik,skrc->sirc") - contract(
        back_sin, came_im, "ik,skrc->sirc"
    )
    result_re = out_re / length
    conv = result_re[0]
    backward = result_re[1]
    lagged = result_re[2]
    gate_grad = (gout_cols.astype(jnp.float32) * (conv + skip * tok_real)).astype(jnp.bfloat16)
    filter_grad = lagged / math.sqrt(blocks * tok_rows)
    token_grad = (backward + skip * grad_real).astype(jnp.bfloat16)
    send_rows = 2 * tok_rows // blocks
    targets = owner.reshape(-1) * send_rows + slot.reshape(-1) - my_index * send_rows
    outbox = (
        jnp.zeros((blocks * send_rows, channels), jnp.bfloat16)
        .at[targets]
        .set(token_grad.reshape(tok_rows, channels))
    )
    inbox = lax.all_to_all(
        outbox.reshape(blocks, send_rows, channels), "bins", split_axis=0, concat_axis=0, tiled=True
    )
    grad_rows = inbox.reshape(blocks * send_rows, channels)
    return (gate_grad, filter_grad, grad_rows)


def solution(mesh):
    return jax.shard_map(
        shards,
        mesh=mesh,
        in_specs=(
            P("bins", "chan"),
            P("bins", "chan"),
            P("bins", "chan"),
            P("chan"),
            P("bins", "chan"),
            P("chan", None),
            P(None, "bins"),
            P(None, "bins"),
        ),
        out_specs=(P(None, "bins", "chan"), P(None, "bins", "chan"), P("bins", "chan")),
        check_vma=False,
    )
```

profile of v0, /device:TPU:1, one launch (start us, length us, event | category | flops | bytes accessed | tf_op | source)
XLA Modules:
  0.0 447.9 jit_solution(11163061509946371895)
XLA Ops:
  7.2 0.7 all-gather.2.cloned.1.call-update
  7.9 8.6 %all-to-all-start.1 = ((bf16[16,32,256]{2,1,0:T(8,128)(2,1)}), bf16[16,32,256]{2,1,0:T(8,128)(2,1)S(1)}, u32[]{:S(2)}, u32[]{:S(2)}) async-start(bf16[16,32,256]{2,1,0:T(8,128)(2,1)} %bitcast.142), calls=%async_computation.1 | async-start | bytes 524288 | tf_op jit(solution)/shard_map/all_to_all | solution.py:60
  16.8 0.2 fusion.61
  16.9 7.1 %all-to-all-done.1 = bf16[16,32,256]{2,1,0:T(8,128)(2,1)S(1)} async-done(((bf16[16,32,256]{2,1,0:T(8,128)(2,1)}), bf16[16,32,256]{2,1,0:T(8,128)(2,1)S(1)}, u32[]{:S(2)}, u32[]{:S(2)}) %all-to-all-start.1) | async-done | bytes 262176 | tf_op jit(solution)/shard_map/all_to_all | solution.py:60
  24.0 3.6 all-to-all-start.2
  27.5 17.8 %all-gather.2.cloned.1.call-done = bf16[512,4096]{1,0:T(8,128)(2,1)} async-done(((bf16[512,512]{1,0:T(8,128)(2,1)}), bf16[512,4096]{1,0:T(8,128)(2,1)}) %all-gather.2.cloned.1.call-update) | async-done | bytes 4194320 | tf_op jit(solution)/shard_map/all_gather | solution.py:51
  45.3 4.3 multiply_convert_fusion
  49.6 7.2 %all-to-all-start.3 = ((bf16[16,32,256]{2,1,0:T(8,128)(2,1)}), bf16[16,32,256]{2,1,0:T(8,128)(2,1)S(1)}, u32[]{:S(2)}, u32[]{:S(2)}) async-start(bf16[16,32,256]{2,1,0:T(8,128)(2,1)} %bitcast.5), calls=%async_computation.3 | async-start | bytes 524288 | tf_op jit(solution)/shard_map/all_to_all | solution.py:66
  56.9 0.2 convert_bitcast_fusion.1
  57.0 0.2 bitcast_convert_fusion
  57.2 7.3 %all-to-all-done.3 = bf16[16,32,256]{2,1,0:T(8,128)(2,1)S(1)} async-done(((bf16[16,32,256]{2,1,0:T(8,128)(2,1)}), bf16[16,32,256]{2,1,0:T(8,128)(2,1)S(1)}, u32[]{:S(2)}, u32[]{:S(2)}) %all-to-all-start.3) | async-done | bytes 262176 | tf_op jit(solution)/shard_map/all_to_all | solution.py:66
  64.5 0.2 convert_bitcast_fusion
  64.6 2.8 fusion.16
  67.4 3.6 fusion.3
  71.1 1.1 pad_maximum_fusion
  72.2 6.3 %copy.48 = f32[3,2,32,32,256]{4,3,0,1,2:T(8,128)} copy(f32[3,2,32,32,256]{4,2,3,0,1:T(8,128)S(1)} %pad_maximum_fusion) | data formatting | bytes 12582912 | tf_op jit(solution)/shard_map/stack | solution.py:79
  78.4 4.8 %all-to-all-start.4 = ((f32[3,2,32,32,256]{4,3,0,1,2:T(8,128)}), f32[3,2,32,32,256]{4,3,0,1,2:T(8,128)}, u32[]{:S(2)}, u32[]{:S(2)}) async-start(f32[3,2,32,32,256]{4,3,0,1,2:T(8,128)} %copy.48), calls=%async_computation.4 | async-start | bytes 12582912 | tf_op jit(solution)/shard_map/all_to_all | solution.py:83
  83.3 0.2 fusion.75
  83.5 96.7 %all-to-all-done.4 = f32[3,2,32,32,256]{4,3,0,1,2:T(8,128)} async-done(((f32[3,2,32,32,256]{4,3,0,1,2:T(8,128)}), f32[3,2,32,32,256]{4,3,0,1,2:T(8,128)}, u32[]{:S(2)}, u32[]{:S(2)}) %all-to-all-start.4) | async-done | bytes 6291488 | tf_op jit(solution)/shard_map/all_to_all | solution.py:83
  180.2 3.5 copy.50
  183.7 14.5 %fusion.7 = f32[3,2,256,512]{3,2,1,0:T(8,128)S(1)} fusion(f32[3,2,2,512,256]{4,3,2,1,0:T(8,128)S(1)} %bitcast.136), kind=kOutput, calls=%fused_computation.24 | convolution fusion | flops 4835508224 | bytes 6291456 | tf_op jit(solution)/shard_map/kr,slrc->slkc/dot_general | solution.py:16
  198.2 14.7 %fusion.6 = f32[3,2,256,512]{3,2,1,0:T(8,128)S(1)} fusion(f32[3,2,2,512,256]{4,3,2,1,0:T(8,128)S(1)} %bitcast.137), kind=kOutput, calls=%fused_computation.23 | convolution fusion | flops 4835508224 | bytes 6291456 | tf_op jit(solution)/shard_map/kr,slrc->slkc/dot_general | solution.py:16
  213.0 14.6 %add_bitcast_fusion.1 = f32[3,2,512,256]{2,3,1,0:T(8,128)S(1)} fusion(f32[3,2,256,512]{3,2,1,0:T(8,128)S(1)} %fusion.7, f32[3,2,2,512,256]{4,3,2,1,0:T(8,128)S(1)} %bitcast.138), kind=kOutput, calls=%fused_computation.22 | convolution fusion | flops 4836294656 | bytes 9437184 | tf_op jit(solution)/shard_map/kr,slrc->slkc/dot_general | solution.py:16
  227.5 14.3 %subtract_bitcast_fusion.1 = f32[3,2,512,256]{2,3,1,0:T(8,128)S(1)} fusion(f32[3,2,256,512]{3,2,1,0:T(8,128)S(1)} %fusion.6, f32[3,2,2,512,256]{4,3,2,1,0:T(8,128)S(1)} %bitcast.139), kind=kOutput, calls=%fused_computation.21 | convolution fusion | flops 4836294656 | bytes 9437184 | tf_op jit(solution)/shard_map/kr,slrc->slkc/dot_general | solution.py:16
  241.9 0.8 multiply_subtract_fusion.1
  242.6 0.8 multiply_subtract_fusion.2
  243.4 9.7 %fusion.10 = f32[3,2,256,512]{3,2,1,0:T(8,128)S(1)} fusion(f32[1,2,512,256]{2,3,1,0:T(8,128)S(1)} %get-tuple-element.22, f32[1,2,512,256]{2,3,1,0:T(8,128)S(1)} %get-tuple-element.21, f32[1,2,512,256]{2,3,1,0:T(8,128)S(1)} %get-tuple-element.24), kind=kOutput, calls=%fused_computation.27 | convolution fusion | flops 4837081088 | bytes 6291456 | tf_op jit(solution)/shard_map/rk,slkc->slrc/dot_general | solution.py:16
  253.1 9.4 %fusion.11 = f32[3,2,256,512]{3,2,1,0:T(8,128)S(1)} fusion(f32[1,2,512,256]{2,3,1,0:T(8,128)S(1)} %get-tuple-element.22, f32[1,2,512,256]{2,3,1,0:T(8,128)S(1)} %get-tuple-element.21, f32[1,2,512,256]{2,3,1,0:T(8,128)S(1)} %get-tuple-element.24), kind=kOutput, calls=%fused_computation.28 | convolution fusion | flops 4837081088 | bytes 6291456 | tf_op jit(solution)/shard_map/rk,slkc->slrc/dot_general | solution.py:16
  262.5 9.7 %fusion.14 = f32[3,2,256,512]{3,2,1,0:T(8,128)S(1)} fusion(f32[3,2,256,512]{3,2,1,0:T(8,128)S(1)} %fusion.11, f32[1,2,512,256]{2,3,1,0:T(8,128)S(1)} %get-tuple-element.20, f32[1,2,512,256]{2,3,1,0:T(8,128)S(1)} %get-tuple-element.23, f32[1,2,512,256]{2,3,1,0:T(8,128)S(1)} %get-tuple-element.19), kind=kOutput, calls=%fused_computation.31 | convolution fusion | flops 4837867520 | bytes 9437184 | tf_op jit(solution)/shard_map/rk,slkc->slrc/dot_general | solution.py:16
  272.3 9.9 %subtract_bitcast_fusion = (f32[3,1,2,512,256]{3,4,2,0,1:T(8,128)S(1)}, f32[3,1,2,512,256]{3,4,2,0,1:T(8,128)S(1)}) fusion(f32[3,2,256,512]{3,2,1,0:T(8,128)S(1)} %fusion.14, f32[2,512]{1,0:T(2,128)S(1)} %get-tuple-element.30, f32[2,512]{1,0:T(2,128)S(1)} %get-tuple-element.29, f32[3,2,256,512]{3,2,1,0:T(8,128)S(1)} %fusion.10, ...), kind=kOutput, calls=%fused_computation.20 | convolution fusion | flops 4842586112 | bytes 15736832 | tf_op jit(solution)/shard_map/rk,slkc->slrc/dot_general | solution.py:16
  282.2 3.5 pad_maximum_fusion.1
  285.7 10.5 %copy.53 = f32[3,2,2,512,256]{4,2,0,1,3:T(2,128)} copy(f32[3,2,2,512,256]{3,4,2,0,1:T(8,128)} %pad_maximum_fusion.1) | data formatting | bytes 12582912 | tf_op jit(solution)/shard_map/stack | solution.py:109
  296.2 7.4 %all-to-all-start.5 = ((f32[3,2,2,512,256]{4,2,0,1,3:T(2,128)}), f32[3,2,2,512,256]{4,2,0,1,3:T(2,128)}, u32[]{:S(2)}, u32[]{:S(2)}) async-start(f32[3,2,2,512,256]{4,2,0,1,3:T(2,128)} %copy.53), calls=%async_computation.5 | async-start | bytes 12582912 | tf_op jit(solution)/shard_map/all_to_all | solution.py:110
  303.7 73.0 %all-to-all-done.5 = f32[3,2,2,512,256]{4,2,0,1,3:T(2,128)} async-done(((f32[3,2,2,512,256]{4,2,0,1,3:T(2,128)}), f32[3,2,2,512,256]{4,2,0,1,3:T(2,128)}, u32[]{:S(2)}, u32[]{:S(2)}) %all-to-all-start.5) | async-done | bytes 6291488 | tf_op jit(solution)/shard_map/all_to_all | solution.py:110
  376.7 8.3 %all-to-all-start = ((bf16[16,32,256]{2,1,0:T(8,128)(2,1)}), bf16[16,32,256]{2,1,0:T(8,128)(2,1)S(1)}, u32[]{:S(2)}, u32[]{:S(2)}) async-start(bf16[16,32,256]{2,1,0:T(8,128)(2,1)} %bitcast), calls=%async_computation | async-start | bytes 524288 | tf_op jit(solution)/shard_map/all_to_all | solution.py:69
  385.0 6.6 %copy.54 = f32[3,2,2,512,256]{4,3,2,1,0:T(8,128)} copy(f32[3,2,2,512,256]{4,2,0,1,3:T(2,128)} %all-to-all-done.5) | data formatting | bytes 12582912 | tf_op jit(solution)/shard_map/all_to_all | solution.py:110
  391.6 10.3 %copy.55 = f32[3,2,16,2,32,256]{5,3,2,4,0,1:T(2,128)} copy(f32[3,2,16,2,32,256]{5,4,2,3,1,0:T(8,128)} %bitcast.140) | data formatting | bytes 12582912 | tf_op jit(solution)/shard_map/all_to_all | solution.py:110
  401.9 8.5 %all_to_all.52 = f32[3,2,32,32,256]{4,2,3,0,1:T(8,128)} reshape(f32[3,2,16,2,32,256]{5,3,2,4,0,1:T(2,128)} %copy.55) | data formatting | bytes 12582912 | tf_op jit(solution)/shard_map/all_to_all | solution.py:110
  410.4 3.7 fusion
  414.1 4.9 %multiply_bitcast_fusion = f32[3,16,32,256]{3,1,2,0:T(8,128)} fusion(f32[3,32,256,16]{2,3,1,0:T(8,128)S(1)} %fusion, f32[3,2,32,32,256]{4,2,3,0,1:T(8,128)} %all_to_all.52, s32[32]{0:T(128)S(1)} %mul.319), kind=kOutput, calls=%fused_computation.34 | convolution fusion | flops 151788544 | bytes 6291584 | tf_op jit(solution)/shard_map/ik,skrc->sirc/dot_general | solution.py:16
  419.0 1.8 fusion.36
  421.0 3.4 scatter_custom_fusion
  424.3 6.7 %all-to-all-start.6 = ((bf16[16,64,256]{2,1,0:T(8,128)(2,1)}), bf16[16,64,256]{2,1,0:T(8,128)(2,1)S(1)}, u32[]{:S(2)}, u32[]{:S(2)}) async-start(bf16[16,64,256]{2,1,0:T(8,128)(2,1)} %bitcast.44), calls=%async_computation.6 | async-start | bytes 1048576 | tf_op jit(solution)/shard_map/all_to_all | solution.py:130
  431.0 1.1 fusion.37
  432.1 1.1 copy.58
  433.2 0.8 copy.57
  434.0 6.1 %all-to-all-done.6 = bf16[16,64,256]{2,1,0:T(8,128)(2,1)S(1)} async-done(((bf16[16,64,256]{2,1,0:T(8,128)(2,1)}), bf16[16,64,256]{2,1,0:T(8,128)(2,1)S(1)}, u32[]{:S(2)}, u32[]{:S(2)}) %all-to-all-start.6) | async-done | bytes 524320 | tf_op jit(solution)/shard_map/all_to_all | solution.py:130
  440.0 0.8 copy.73
  (24 shorter events, 0.5 us)
Async XLA Ops:
  7.2 38.2 %copy-start = (bf16[256,4096]{1,0:T(8,128)(2,1)S(1)}, bf16[256,4096]{1,0:T(8,128)(2,1)}, u32[]{:S(2)}) copy-start(bf16[256,4096]{1,0:T(8,128)(2,1)} %param.13) | copy-start | bytes 6291460
  7.2 38.1 %all-gather.2.cloned.1.call-start = ((), (), s32[]{:S(2)}) async-start(), calls=%async_computation.7 | async-start | bytes 4718592 | tf_op jit(solution)/shard_map/all_gather | solution.py:51
  7.9 16.1 %all-to-all-start.1 = ((bf16[16,32,256]{2,1,0:T(8,128)(2,1)}), bf16[16,32,256]{2,1,0:T(8,128)(2,1)S(1)}, u32[]{:S(2)}, u32[]{:S(2)}) async-start(bf16[16,32,256]{2,1,0:T(8,128)(2,1)} %bitcast.142), calls=%async_computation.1 | async-start | bytes 524288 | tf_op jit(solution)/shard_map/all_to_all | solution.py:60
  24.0 25.6 %all-to-all-start.2 = ((bf16[16,32,256]{2,1,0:T(8,128)(2,1)}), bf16[16,32,256]{2,1,0:T(8,128)(2,1)S(1)}, u32[]{:S(2)}, u32[]{:S(2)}) async-start(bf16[16,32,256]{2,1,0:T(8,128)(2,1)} %bitcast.143), calls=%async_computation.2 | async-start | bytes 524288 | tf_op jit(solution)/shard_map/all_to_all | solution.py:63
  49.6 14.9 %all-to-all-start.3 = ((bf16[16,32,256]{2,1,0:T(8,128)(2,1)}), bf16[16,32,256]{2,1,0:T(8,128)(2,1)S(1)}, u32[]{:S(2)}, u32[]{:S(2)}) async-start(bf16[16,32,256]{2,1,0:T(8,128)(2,1)} %bitcast.5), calls=%async_computation.3 | async-start | bytes 524288 | tf_op jit(solution)/shard_map/all_to_all | solution.py:66
  78.4 101.7 %all-to-all-start.4 = ((f32[3,2,32,32,256]{4,3,0,1,2:T(8,128)}), f32[3,2,32,32,256]{4,3,0,1,2:T(8,128)}, u32[]{:S(2)}, u32[]{:S(2)}) async-start(f32[3,2,32,32,256]{4,3,0,1,2:T(8,128)} %copy.48), calls=%async_computation.4 | async-start | bytes 12582912 | tf_op jit(solution)/shard_map/all_to_all | solution.py:83
  296.2 7.4 %copy-start.2 = (s32[16,32]{1,0:T(8,128)S(1)}, s32[16,32]{1,0:T(8,128)}, u32[]{:S(2)}) copy-start(s32[16,32]{1,0:T(8,128)} %param.15) | copy-start | bytes 6148
  296.2 7.4 %copy-start.3 = (s32[16,32]{1,0:T(8,128)S(1)}, s32[16,32]{1,0:T(8,128)}, u32[]{:S(2)}) copy-start(s32[16,32]{1,0:T(8,128)} %param.14) | copy-start | bytes 6148
  296.2 80.5 %all-to-all-start.5 = ((f32[3,2,2,512,256]{4,2,0,1,3:T(2,128)}), f32[3,2,2,512,256]{4,2,0,1,3:T(2,128)}, u32[]{:S(2)}, u32[]{:S(2)}) async-start(f32[3,2,2,512,256]{4,2,0,1,3:T(2,128)} %copy.53), calls=%async_computation.5 | async-start | bytes 12582912 | tf_op jit(solution)/shard_map/all_to_all | solution.py:110
  376.7 42.4 %all-to-all-start = ((bf16[16,32,256]{2,1,0:T(8,128)(2,1)}), bf16[16,32,256]{2,1,0:T(8,128)(2,1)S(1)}, u32[]{:S(2)}, u32[]{:S(2)}) async-start(bf16[16,32,256]{2,1,0:T(8,128)(2,1)} %bitcast), calls=%async_computation | async-start | bytes 524288 | tf_op jit(solution)/shard_map/all_to_all | solution.py:69
  414.1 4.9 %copy-start.4 = (f32[256]{0:T(256)S(1)}, f32[256]{0:T(256)}, u32[]{:S(2)}) copy-start(f32[256]{0:T(256)} %param.11) | copy-start | bytes 3076
  419.0 21.8 %copy-start.1 = (bf16[256,4096]{1,0:T(8,128)(2,1)S(1)}, bf16[256,4096]{1,0:T(8,128)(2,1)}, u32[]{:S(2)}) copy-start(bf16[256,4096]{1,0:T(8,128)(2,1)} %param.13) | copy-start | bytes 6291460
  424.3 15.7 %all-to-all-start.6 = ((bf16[16,64,256]{2,1,0:T(8,128)(2,1)}), bf16[16,64,256]{2,1,0:T(8,128)(2,1)S(1)}, u32[]{:S(2)}, u32[]{:S(2)}) async-start(bf16[16,64,256]{2,1,0:T(8,128)(2,1)} %bitcast.44), calls=%async_computation.6 | async-start | bytes 1048576 | tf_op jit(solution)/shard_map/all_to_all | solution.py:130
Sparse Core Ops, SparseCore 0:
  9.7 35.5 all-gather.1
where the time goes:
time: 456 us; the launch traced here: 448 us
  waiting for transfers between devices  209 us (46%)
  matrix products  116 us (25%)
  local copies, waits for them, and re-layouts  52.1 us (11%)
  starting transfers between devices  46.6 us (10%)
  between operations  14.5 us (3%)
  other arithmetic  9.98 us (2%)
    dot_general x12, matrix products, contract(): return jnp.einsum(form, table, values, precision=exact_mode)  112 us
    all_to_all x1, waiting for transfers between devices, shards(): lax.all_to_all(turned, 'bins', split_axis=2, concat_axis=3, tiled=True)  96.7 us
    all_to_all x1, waiting for transfers between devices, shards(): lax.all_to_all(turned, 'bins', split_axis=3, concat_axis=2, tiled=True)  73 us
    all_to_all x3, local copies, waits for them, and re-layouts, shards(): lax.all_to_all(turned, 'bins', split_axis=3, concat_axis=2, tiled=True)  25.4 us
    all_gather x1, waiting for transfers between devices, shards(): lax.all_gather(out_grad, 'chan', axis=1, tiled=True)  17.8 us
    another operation x1, local copies, waits for them, and re-layouts, shards(): turned = jnp.stack([twist_re, twist_im], axis=1)  10.5 us
  transfers between devices with their start and end apart: 8, of which 6 were waited for; matrix products, arithmetic and copies ran while one was open for 8% of the time, Pallas kernels for 0%

commit v1 on v0

v1 whole, which is shorter than its diff:
```python
import functools
import math

import jax
import jax.numpy as jnp
import numpy as np
from jax import lax
from jax.experimental import pallas as pl
from jax.experimental.pallas import tpu as pltpu
from jax.sharding import PartitionSpec as P

BLOCKS = 16
HELD = 16
ROWS = 512
HALF = BLOCKS + 1
LENGTH = 2 * BLOCKS * ROWS


def tables():
    k1 = np.arange(HALF)
    i = np.arange(BLOCKS)
    ang = 2.0 * np.pi * np.outer(k1, i) / (2 * BLOCKS)
    eye = np.eye(HELD)
    ahead = np.concatenate([np.kron(np.cos(ang), eye), np.kron(-np.sin(ang), eye)], axis=0)
    weight = np.where((k1 == 0) | (k1 == BLOCKS), 1.0, 2.0)[None, :] / LENGTH
    back_re = np.kron(weight * np.cos(ang).T, eye)
    back_im = np.kron(-(weight * np.sin(ang).T)[:, 1:BLOCKS], eye)
    back = np.concatenate([back_re, back_im], axis=1)
    r = np.arange(ROWS)
    twist = 2.0 * np.pi * np.outer(k1, r) / LENGTH
    inner = 2.0 * np.pi * (np.outer(r, r) % ROWS) / ROWS
    return (
        jnp.asarray(ahead, jnp.bfloat16),
        jnp.asarray(back, jnp.bfloat16),
        jnp.asarray(np.cos(twist)[:, None, :], jnp.float32),
        jnp.asarray(np.sin(twist)[:, None, :], jnp.float32),
        jnp.asarray(np.cos(inner), jnp.bfloat16),
        jnp.asarray(np.sin(inner), jnp.bfloat16),
    )


def mm(a, b):
    return jnp.dot(a, b, preferred_element_type=jnp.float32)


def stage_rows(value):
    return value.reshape(HALF, HELD, ROWS)


def flat(value):
    return value.reshape(HALF * HELD, ROWS)


def forward(value, ahead, tw_cos, tw_sin, in_cos, in_sin):
    part = mm(ahead, value)
    n = HALF * HELD
    re, im = stage_rows(part[:n]), stage_rows(part[n:])
    z_re = flat(re * tw_cos + im * tw_sin)
    z_im = flat(im * tw_cos - re * tw_sin)
    z = jnp.concatenate([z_re, z_im], axis=0).astype(jnp.bfloat16)
    by_cos, by_sin = mm(z, in_cos), mm(z, in_sin)
    return by_cos[:n] + by_sin[n:], by_cos[n:] - by_sin[:n]


def inverse(s_re, s_im, back, tw_cos, tw_sin, in_cos, in_sin):
    n = HALF * HELD
    q = jnp.concatenate([s_re, s_im], axis=0).astype(jnp.bfloat16)
    by_cos, by_sin = mm(q, in_cos), mm(q, in_sin)
    re, im = stage_rows(by_cos[:n] - by_sin[n:]), stage_rows(by_cos[n:] + by_sin[:n])
    t_re = flat(re * tw_cos - im * tw_sin)
    t_im = flat(im * tw_cos + re * tw_sin)[HELD : BLOCKS * HELD]
    t = jnp.concatenate([t_re, t_im], axis=0).astype(jnp.bfloat16)
    return mm(back, t)


def to_columns(value):
    group = lax.broadcasted_iota(jnp.int32, (HELD, 128), 1) // 32
    out = [[None] * 4 for _ in range(BLOCKS)]
    for i_hi in range(4):
        for j_hi in range(4):
            tiles = [
                value[(4 * i_hi + i_lo) * HELD : (4 * i_hi + i_lo + 1) * HELD, 128 * j_hi : 128 * (j_hi + 1)]
                for i_lo in range(4)
            ]
            for j_lo in range(4):
                acc = None
                for i_lo in range(4):
                    shift = (32 * (i_lo - j_lo)) % 128
                    turned = pltpu.roll(tiles[i_lo], shift, 1) if shift else tiles[i_lo]
                    acc = turned if acc is None else jnp.where(group == i_lo, turned, acc)
                out[4 * j_hi + j_lo][i_hi] = acc
    return jnp.concatenate([jnp.concatenate(row, axis=1) for row in out], axis=0)


def transform_kernel(
    x_ref, h_ref, gate_ref, g_ref, skip_ref, ahead, back, tw_cos, tw_sin, in_cos, in_sin, out_ref
):
    f32 = jnp.float32
    forward_tables = (ahead[...], tw_cos[...], tw_sin[...], in_cos[...], in_sin[...])
    inverse_tables = (back[...], tw_cos[...], tw_sin[...], in_cos[...], in_sin[...])
    x = x_ref[...]
    skip = skip_ref[...]
    x_re, x_im = forward(x, *forward_tables)
    h_re, h_im = forward(h_ref[...], *forward_tables)
    conv = inverse(x_re * h_re - x_im * h_im, x_re * h_im + x_im * h_re, *inverse_tables)
    g = g_ref[...].astype(f32)
    out_ref[0] = to_columns(g * (conv + skip * x.astype(f32))).astype(jnp.bfloat16)
    dy = (g * gate_ref[...].astype(f32)).astype(jnp.bfloat16)
    y_re, y_im = forward(dy, *forward_tables)
    grad = inverse(h_re * y_re + h_im * y_im, h_re * y_im - h_im * y_re, *inverse_tables)
    out_ref[1] = to_columns(grad + skip * dy.astype(f32)).astype(jnp.bfloat16)
    lag = inverse(y_re * x_re + y_im * x_im, y_im * x_re - y_re * x_im, *inverse_tables)
    out_ref[2] = to_columns(lag * (1.0 / math.sqrt(BLOCKS * ROWS))).astype(jnp.bfloat16)


def transform(x, h, gate, g, skip):
    return pl.pallas_call(
        transform_kernel,
        out_shape=jax.ShapeDtypeStruct((3, BLOCKS * HELD, ROWS), jnp.bfloat16),
        compiler_params=pltpu.CompilerParams(vmem_limit_bytes=48 << 20),
    )(x, h, gate, g, skip, *tables())


def shards(tokens_in, filters, gate, skip, out_grad, out_weight, owner, slot):
    my_index = lax.axis_index("bins")
    channels = tokens_in.shape[1]

    def spread(value):
        return lax.all_to_all(value, "bins", split_axis=0, concat_axis=0, tiled=True)

    early = jnp.stack([v.T.reshape(BLOCKS, HELD, ROWS) for v in (tokens_in, filters, gate)], axis=1)
    early = spread(early)
    upstream = lax.dot_general(
        out_weight,
        lax.all_gather(out_grad, "chan", axis=1, tiled=True),
        (((1,), (1,)), ((), ())),
        preferred_element_type=jnp.float32,
    ).astype(jnp.bfloat16)
    g = spread(upstream.reshape(BLOCKS, HELD, ROWS)).reshape(BLOCKS * HELD, ROWS)
    x, h, gates = (early[:, n].reshape(BLOCKS * HELD, ROWS) for n in range(3))
    own_skip = jnp.tile(lax.dynamic_slice_in_dim(skip, my_index * HELD, HELD), BLOCKS)[:, None]
    done = transform(x, h, gates, g, own_skip)
    done = spread(done.reshape(3, BLOCKS, HELD, ROWS).transpose(1, 0, 2, 3))
    gate_grad, token_grad, filter_grad = (done[:, n].reshape(channels, ROWS) for n in range(3))
    gate_grad = gate_grad.T.reshape(BLOCKS, ROWS // BLOCKS, channels)
    filter_grad = filter_grad.T.reshape(BLOCKS, ROWS // BLOCKS, channels).astype(jnp.float32)
    send_rows = 2 * ROWS // BLOCKS
    targets = owner.reshape(1, -1) * send_rows + slot.reshape(1, -1) - my_index * send_rows
    places = lax.broadcasted_iota(jnp.int32, (BLOCKS * send_rows, ROWS), 0)
    chosen = (places == targets).astype(jnp.bfloat16)
    outbox = lax.dot_general(
        chosen, token_grad, (((1,), (1,)), ((), ())), preferred_element_type=jnp.float32
    ).astype(jnp.bfloat16)
    inbox = spread(outbox.reshape(BLOCKS, send_rows, channels))
    return (gate_grad, filter_grad, inbox.reshape(BLOCKS * send_rows, channels))


def solution(mesh):
    return jax.shard_map(
        shards,
        mesh=mesh,
        in_specs=(
            P("bins", "chan"),
            P("bins", "chan"),
            P("bins", "chan"),
            P("chan"),
            P("bins", "chan"),
            P("chan", None),
            P(None, "bins"),
            P(None, "bins"),
        ),
        out_specs=(P(None, "bins", "chan"), P(None, "bins", "chan"), P("bins", "chan")),
        check_vma=False,
    )
```

time: 456 us -> 118 us (0.26)
  the two profiles are of different devices: /device:TPU:1 before, /device:TPU:0 now
where the time goes in v1:
time: 118 us; the launch traced here: 117 us
  waiting for transfers between devices  53.8 us (46%)
  starting transfers between devices  22.4 us (19%)
  local copies, waits for them, and re-layouts  14.7 us (12%)
  between operations  14.2 us (12%)
  Pallas kernels  6.12 us (5%)
  matrix products  5.47 us (5%)
    all_to_all x4, waiting for transfers between devices, spread(): lax.all_to_all(value, 'bins', split_axis=0, concat_axis=0, tiled=True)  29.5 us
    all_gather x1, waiting for transfers between devices, shards(): lax.all_gather(out_grad, 'chan', axis=1, tiled=True)  23.6 us
    all_to_all x4, starting transfers between devices, spread(): lax.all_to_all(value, 'bins', split_axis=0, concat_axis=0, tiled=True)  22.3 us
    unnamed x26, local copies, waits for them, and re-layouts  9.54 us
    pallas_call x1, Pallas kernels, transform(): pl.pallas_call(transform_kernel, out_shape=jax.ShapeDtypeStruct((3, BLOCK...  6.12 us
    dot_general x1, matrix products, shards(): lax.dot_general(out_weight, lax.all_gather(out_grad, 'chan', axis=1, tile...  4.18 us
  transfers between devices with their start and end apart: 5, of which 4 were waited for; matrix products, arithmetic and copies ran while one was open for 10% of the time, Pallas kernels for 0%

profile of v1, /device:TPU:0, one launch (start us, length us, event | category | flops | bytes accessed | tf_op | source)
XLA Modules:
  0.0 116.8 jit_solution(1823700654444085363)
XLA Ops:
  7.2 0.0 copy-start
  7.2 0.0 all-gather.2.cloned.1.call-start
  7.2 0.7 all-gather.2.cloned.1.call-update
  7.9 1.1 copy.28
  9.0 1.1 copy.29
  10.1 1.1 copy.30
  11.2 0.0 copy-start.10
  11.2 0.1 pad_maximum_fusion
  11.3 0.9 copy.31
  12.2 8.2 %all-to-all-start = ((bf16[16,3,16,512]{3,2,1,0:T(8,128)(2,1)}), bf16[16,3,16,512]{3,2,1,0:T(8,128)(2,1)S(1)}, u32[]{:S(2)}, u32[]{:S(2)}) async-start(bf16[16,3,16,512]{3,2,1,0:T(8,128)(2,1)} %copy.31), calls=%async_computation | async-start | bytes 1572864 | tf_op jit(solution)/shard_map/all_to_all | solution.py:129
  20.4 0.0 copy-done.10
  20.4 0.1 dynamic_slice.3
  20.5 0.1 broadcast_in_dim_tile.4.skip_ref
  20.6 23.6 %all-gather.2.cloned.1.call-done = bf16[512,4096]{1,0:T(8,128)(2,1)} async-done(((bf16[512,512]{1,0:T(8,128)(2,1)}), bf16[512,4096]{1,0:T(8,128)(2,1)}) %all-gather.2.cloned.1.call-update) | async-done | bytes 4194320 | tf_op jit(solution)/shard_map/all_gather | solution.py:135
  44.2 0.0 copy-done
  44.2 4.2 %convolution_convert_fusion = bf16[256,512]{1,0:T(8,128)(2,1)} fusion(bf16[256,4096]{1,0:T(8,128)(2,1)S(1)} %copy-done, bf16[512,4096]{1,0:T(8,128)(2,1)} %all-gather.2.cloned.1.call-done), kind=kOutput, calls=%fused_computation.3 | convolution fusion | flops 1073872896 | bytes 6553600 | tf_op jit(solution)/shard_map/dot_general | solution.py:133
  48.4 0.0 copy-start.3
  48.4 0.0 all-to-all-done
  48.4 0.0 copy-start.7
  48.4 0.9 copy-done.7
  49.3 7.0 %all-to-all-start.1 = ((bf16[16,16,512]{2,1,0:T(8,128)(2,1)}), bf16[16,16,512]{2,1,0:T(8,128)(2,1)S(1)}, u32[]{:S(2)}, u32[]{:S(2)}) async-start(bf16[16,16,512]{2,1,0:T(8,128)(2,1)} %bitcast.9), calls=%async_computation.1 | async-start | bytes 524288 | tf_op jit(solution)/shard_map/all_to_all | solution.py:129
  56.3 1.2 %fusion.4 = (bf16[16,1,16,512]{3,2,1,0:T(8,128)(2,1)S(1)}, bf16[16,1,16,512]{3,2,1,0:T(8,128)(2,1)S(1)}, bf16[16,1,16,512]{3,2,1,0:T(8,128)(2,1)S(1)}) fusion(bf16[16,3,16,512]{3,2,1,0:T(8,128)(2,1)} %copy-done.7), kind=kLoop, calls=%fused_computation.10 | loop fusion | bytes 1572864 | tf_op jit(solution)/shard_map/slice | solution.py:140
  57.5 7.7 %all-to-all-done.1 = bf16[16,16,512]{2,1,0:T(8,128)(2,1)S(1)} async-done(((bf16[16,16,512]{2,1,0:T(8,128)(2,1)}), bf16[16,16,512]{2,1,0:T(8,128)(2,1)S(1)}, u32[]{:S(2)}, u32[]{:S(2)}) %all-to-all-start.1) | async-done | bytes 262176 | tf_op jit(solution)/shard_map/all_to_all | solution.py:129
  65.2 0.0 copy-done.3
  65.2 0.0 copy-start.1
  65.2 1.0 copy-done.1
  66.2 0.0 copy-start.2
  66.2 1.0 copy-done.2
  67.3 0.9 copy-done.4
  68.2 0.8 copy-done.5
  69.0 0.8 copy-done.6
  69.7 6.1 %shard_map.157 = bf16[3,256,512]{2,1,0:T(8,128)(2,1)S(1)} custom-call(bf16[256,512]{1,0:T(8,128)(2,1)S(1)} %bitcast.38, bf16[256,512]{1,0:T(8,128)(2,1)S(1)} %bitcast.37, bf16[256,512]{1,0:T(8,128)(2,1)S(1)} %bitcast.36, bf16[256,512]{1,0:T(8,128)(2,1)S(1)} %bitcast.35, f32[256,1]{1,0:T(8,128)S(1)} %broadcast_in_dim_tile.4.skip_ref, ...), custom_call_target="tpu_custom_call" | custom-call | tf_op jit(solution)/shard_map/pallas_call | solution.py:117
  75.9 0.0 copy-start.8
  75.9 0.0 copy-start.9
  75.9 0.9 copy.37
  76.8 3.6 %all-to-all-start.2 = ((bf16[16,3,16,512]{3,2,1,0:T(8,128)(2,1)}), bf16[16,3,16,512]{3,2,1,0:T(8,128)(2,1)S(1)}, u32[]{:S(2)}, u32[]{:S(2)}) async-start(bf16[16,3,16,512]{3,2,1,0:T(8,128)(2,1)} %bitcast.39), calls=%async_computation.2 | async-start | bytes 1572864 | tf_op jit(solution)/shard_map/all_to_all | solution.py:129
  80.5 0.0 copy-done.8
  80.5 0.0 copy-done.9
  80.5 0.1 sub.16
  80.6 13.4 %all-to-all-done.2 = bf16[16,3,16,512]{3,2,1,0:T(8,128)(2,1)S(1)} async-done(((bf16[16,3,16,512]{3,2,1,0:T(8,128)(2,1)}), bf16[16,3,16,512]{3,2,1,0:T(8,128)(2,1)S(1)}, u32[]{:S(2)}, u32[]{:S(2)}) %all-to-all-start.2) | async-done | bytes 786464 | tf_op jit(solution)/shard_map/all_to_all | solution.py:129
  94.0 0.1 fusion.3
  94.1 1.3 %fusion.1 = bf16[1024,256]{1,0:T(8,128)(2,1)} fusion(bf16[256,512]{1,0:T(8,128)(2,1)S(1)} %bitcast.48, s32[512]{0:T(512)S(1)} %sub.16), kind=kOutput, calls=%fused_computation.2 | convolution fusion | flops 269221888 | bytes 788480 | tf_op jit(solution)/shard_map/dot_general | solution.py:151
  95.4 3.6 %all-to-all-start.3 = ((bf16[16,64,256]{2,1,0:T(8,128)(2,1)}), bf16[16,64,256]{2,1,0:T(8,128)(2,1)S(1)}, u32[]{:S(2)}, u32[]{:S(2)}) async-start(bf16[16,64,256]{2,1,0:T(8,128)(2,1)} %bitcast.46), calls=%async_computation.3 | async-start | bytes 1048576 | tf_op jit(solution)/shard_map/all_to_all | solution.py:129
  99.0 0.8 copy.34
  99.8 0.1 convert_bitcast_fusion
  99.9 1.0 copy.35
  100.9 8.3 %all-to-all-done.3 = bf16[16,64,256]{2,1,0:T(8,128)(2,1)S(1)} async-done(((bf16[16,64,256]{2,1,0:T(8,128)(2,1)}), bf16[16,64,256]{2,1,0:T(8,128)(2,1)S(1)}, u32[]{:S(2)}, u32[]{:S(2)}) %all-to-all-start.3) | async-done | bytes 524320 | tf_op jit(solution)/shard_map/all_to_all | solution.py:129
  109.2 0.8 copy.39
  (5 shorter events, 0.0 us)
Async XLA Ops:
  7.2 37.1 %copy-start = (bf16[256,4096]{1,0:T(8,128)(2,1)S(1)}, bf16[256,4096]{1,0:T(8,128)(2,1)}, u32[]{:S(2)}) copy-start(bf16[256,4096]{1,0:T(8,128)(2,1)} %param.19) | copy-start | bytes 6291460
  7.2 37.0 %all-gather.2.cloned.1.call-start = ((), (), s32[]{:S(2)}) async-start(), calls=%async_computation.4 | async-start | bytes 4718592 | tf_op jit(solution)/shard_map/all_gather | solution.py:135
  11.2 9.2 %copy-start.10 = (f32[256]{0:T(256)S(1)}, f32[256]{0:T(256)}, u32[]{:S(2)}) copy-start(f32[256]{0:T(256)} %param.17) | copy-start | bytes 3076
  12.2 36.2 %all-to-all-start = ((bf16[16,3,16,512]{3,2,1,0:T(8,128)(2,1)}), bf16[16,3,16,512]{3,2,1,0:T(8,128)(2,1)S(1)}, u32[]{:S(2)}, u32[]{:S(2)}) async-start(bf16[16,3,16,512]{3,2,1,0:T(8,128)(2,1)} %copy.31), calls=%async_computation | async-start | bytes 1572864 | tf_op jit(solution)/shard_map/all_to_all | solution.py:129
  48.4 16.8 %copy-start.3 = (bf16[544,256]{1,0:T(8,128)(2,1)S(1)}, bf16[544,256]{1,0:T(8,128)(2,1)}, u32[]{:S(2)}) copy-start(bf16[544,256]{1,0:T(8,128)(2,1)} %constant.27.clone.ahead) | copy-start | bytes 835588
  48.4 0.9 copy-start.7
  49.3 15.9 %all-to-all-start.1 = ((bf16[16,16,512]{2,1,0:T(8,128)(2,1)}), bf16[16,16,512]{2,1,0:T(8,128)(2,1)S(1)}, u32[]{:S(2)}, u32[]{:S(2)}) async-start(bf16[16,16,512]{2,1,0:T(8,128)(2,1)} %bitcast.9), calls=%async_computation.1 | async-start | bytes 524288 | tf_op jit(solution)/shard_map/all_to_all | solution.py:129
  65.2 1.0 copy-start.1
  66.2 1.0 copy-start.2
  67.3 0.9 copy-start.4
  68.2 0.8 copy-start.5
  69.0 0.8 copy-start.6
  75.9 4.6 %copy-start.8 = (s32[16,32]{1,0:T(8,128)S(1)}, s32[16,32]{1,0:T(8,128)}, u32[]{:S(2)}) copy-start(s32[16,32]{1,0:T(8,128)} %param.21) | copy-start | bytes 6148
  75.9 4.6 %copy-start.9 = (s32[16,32]{1,0:T(8,128)S(1)}, s32[16,32]{1,0:T(8,128)}, u32[]{:S(2)}) copy-start(s32[16,32]{1,0:T(8,128)} %param.20) | copy-start | bytes 6148
  76.8 17.2 %all-to-all-start.2 = ((bf16[16,3,16,512]{3,2,1,0:T(8,128)(2,1)}), bf16[16,3,16,512]{3,2,1,0:T(8,128)(2,1)S(1)}, u32[]{:S(2)}, u32[]{:S(2)}) async-start(bf16[16,3,16,512]{3,2,1,0:T(8,128)(2,1)} %bitcast.39), calls=%async_computation.2 | async-start | bytes 1572864 | tf_op jit(solution)/shard_map/all_to_all | solution.py:129
  95.4 13.8 %all-to-all-start.3 = ((bf16[16,64,256]{2,1,0:T(8,128)(2,1)}), bf16[16,64,256]{2,1,0:T(8,128)(2,1)S(1)}, u32[]{:S(2)}, u32[]{:S(2)}) async-start(bf16[16,64,256]{2,1,0:T(8,128)(2,1)} %bitcast.46), calls=%async_computation.3 | async-start | bytes 1048576 | tf_op jit(solution)/shard_map/all_to_all | solution.py:129
Sparse Core Ops, SparseCore 0:
  9.7 34.4 all-gather.1

commit v2 on v1

--- a/solution.py
+++ b/solution.py
@@ -92,67 +92,297 @@
     return jnp.concatenate([jnp.concatenate(row, axis=1) for row in out], axis=0)
 
 
-def transform_kernel(
-    x_ref, h_ref, gate_ref, g_ref, skip_ref, ahead, back, tw_cos, tw_sin, in_cos, in_sin, out_ref
-):
+def transform_kernel(early_ref, g_ref, skip_ref, ahead, back, tw_cos, tw_sin, in_cos, in_sin, out_ref):
     f32 = jnp.float32
     forward_tables = (ahead[...], tw_cos[...], tw_sin[...], in_cos[...], in_sin[...])
     inverse_tables = (back[...], tw_cos[...], tw_sin[...], in_cos[...], in_sin[...])
-    x = x_ref[...]
+    rows = BLOCKS * HELD
+    x = early_ref[:, 0].reshape(rows, ROWS)
     skip = skip_ref[...]
     x_re, x_im = forward(x, *forward_tables)
-    h_re, h_im = forward(h_ref[...], *forward_tables)
+    h_re, h_im = forward(early_ref[:, 1].reshape(rows, ROWS), *forward_tables)
     conv = inverse(x_re * h_re - x_im * h_im, x_re * h_im + x_im * h_re, *inverse_tables)
-    g = g_ref[...].astype(f32)
-    out_ref[0] = to_columns(g * (conv + skip * x.astype(f32))).astype(jnp.bfloat16)
-    dy = (g * gate_ref[...].astype(f32)).astype(jnp.bfloat16)
+    g = jnp.concatenate([g_ref[0].reshape(rows, ROWS // 2), g_ref[1].reshape(rows, ROWS // 2)], axis=1)
+    g = g.astype(f32)
+    gate = early_ref[:, 2].reshape(rows, ROWS).astype(f32)
+
+    def put(n, value):
+        out_ref[n] = to_columns(value).astype(jnp.bfloat16).reshape(BLOCKS, HELD, ROWS)
+
+    put(2, g * (conv + skip * x.astype(f32)))
+    dy = (g * gate).astype(jnp.bfloat16)
     y_re, y_im = forward(dy, *forward_tables)
     grad = inverse(h_re * y_re + h_im * y_im, h_re * y_im - h_im * y_re, *inverse_tables)
-    out_ref[1] = to_columns(grad + skip * dy.astype(f32)).astype(jnp.bfloat16)
+    put(0, grad + skip * dy.astype(f32))
     lag = inverse(y_re * x_re + y_im * x_im, y_im * x_re - y_re * x_im, *inverse_tables)
-    out_ref[2] = to_columns(lag * (1.0 / math.sqrt(BLOCKS * ROWS))).astype(jnp.bfloat16)
-
-
-def transform(x, h, gate, g, skip):
+    put(1, lag * (1.0 / math.sqrt(BLOCKS * ROWS)))
+
+
+def transform(early, g, skip):
     return pl.pallas_call(
         transform_kernel,
-        out_shape=jax.ShapeDtypeStruct((3, BLOCKS * HELD, ROWS), jnp.bfloat16),
+        out_shape=jax.ShapeDtypeStruct((3, BLOCKS, HELD, ROWS), jnp.bfloat16),
         compiler_params=pltpu.CompilerParams(vmem_limit_bytes=48 << 20),
-    )(x, h, gate, g, skip, *tables())
+    )(early, g, skip, *tables())
+
+
+def remote(src, dst, send, recv, bins, chan):
+    return pltpu.make_async_remote_copy(
+        src_ref=src,
+        dst_ref=dst,
+        send_sem=send,
+        recv_sem=recv,
+        device_id=(bins, chan),
+        device_id_type=pl.DeviceIdType.MESH,
+    )
+
+
+def each(first, last, body):
+    def step(p, carry):
+        body(p)
+        return carry
+
+    lax.fori_loop(first, last, step, 0)
+
+
+def front_kernel(
+    x_ref, h_ref, gate_ref, og_hbm, w_hbm, early_out, g_out,
+    w_all, og_all, acc, early_src, g_src,
+    local_sem, w_sem, mate_sem, side_send, side_recv, far_send, far_recv, early_send, early_recv, g_send, g_recv,
+):
+    b = lax.axis_index("bins")
+    k = lax.axis_index("chan")
+    chip, core = lax.div(k, 2), lax.rem(k, 2)
+    right, left, across = lax.rem(chip + 1, 4), lax.rem(chip + 3, 4), lax.rem(chip + 2, 4)
+    mate = 2 * chip + 1 - core
+
+    own_w = pltpu.make_async_copy(w_hbm, w_all.at[core], local_sem.at[0])
+    own_w.start()
+    own_og = pltpu.make_async_copy(og_hbm.at[core], og_all.at[k], local_sem.at[1])
+    own_og.start()
+
+    barrier = pltpu.get_barrier_semaphore()
+
+    def greet(bins, chan):
+        pl.semaphore_signal(barrier, inc=1, device_id=(bins, chan), device_id_type=pl.DeviceIdType.MESH)
+
+    each(1, BLOCKS, lambda p: greet(lax.rem(b + p, BLOCKS), k))
+    each(0, BLOCKS, lambda p: greet(lax.rem(b + p, BLOCKS), mate))
+    for side in (right, left):
+        for c in range(2):
+            greet(b, 2 * side + c)
+    pl.semaphore_wait(barrier, 2 * BLOCKS - 1 + 4)
+
+    def side_copy(way, part, c):
+        to = (right, left)[way]
+        return remote(
+            og_hbm.at[c, part], og_all.at[k, part],
+            side_send.at[way, part, c], side_recv.at[way, part, core], b, 2 * to + c,
+        )
+
+    for turn in range(2):
+        for c in range(2):
+            side_copy(0, turn, c).start()
+            side_copy(1, 1 - turn, c).start()
+    mate_og = remote(og_hbm.at[1 - core], og_all.at[k], mate_sem.at[0], mate_sem.at[1], b, mate)
+    mate_og.start()
+    mate_w = remote(w_hbm, w_all.at[core], w_sem.at[0], w_sem.at[1], b, mate)
+    mate_w.start()
+
+    for n, ref in enumerate((x_ref, h_ref, gate_ref)):
+        early_src[:, n] = ref[...].T.reshape(BLOCKS, HELD, ROWS)
+
+    def early_copy(p):
+        to = lax.rem(b + p, BLOCKS)
+        return remote(early_src.at[to], early_out.at[b], early_send.at[p], early_recv.at[p], to, k)
+
+    each(1, BLOCKS, lambda p: early_copy(p).start())
+    own_early = pltpu.make_async_copy(early_src.at[b], early_out.at[b], local_sem.at[2])
+    own_early.start()
+
+    def side_arrived(way, part, c):
+        src = 2 * (left, right)[way] + c
+        return remote(
+            og_hbm.at[c, part], og_all.at[src, part],
+            side_send.at[way, part, c], side_recv.at[way, part, c], b, mate,
+        )
+
+    def far_copy(way, c):
+        src = 2 * (left, right)[way] + c
+        to = (right, left)[way]
+        return remote(
+            og_all.at[src, way], og_all.at[src, way],
+            far_send.at[way, c], far_recv.at[way, c], b, 2 * to + core,
+        )
+
+    for c in range(2):
+        for way in range(2):
+            side_arrived(way, way, c).wait_recv()
+            far_copy(way, c).start()
+
+    def gather(source, first=False):
+        columns = pl.ds(pl.multiple_of(source * ROWS, ROWS), ROWS)
+        weights = w_all[:, :, columns].reshape(2 * BLOCKS * HELD, ROWS)
+        term = lax.dot_general(
+            weights, og_all[source].reshape(ROWS // 2, ROWS), (((1,), (1,)), ((), ())),
+            preferred_element_type=jnp.float32,
+        )
+        acc[...] = term if first else acc[...] + term
+
+    own_w.wait()
+    own_og.wait()
+    mate_w.wait()
+    mate_og.wait()
+    gather(k, True)
+    gather(mate)
+    for c in range(2):
+        for way in range(2):
+            side_arrived(way, 1 - way, c).wait_recv()
+            gather(2 * (left, right)[way] + c)
+    for c in range(2):
+        for way in range(2):
+            far_copy(way, c).wait_recv()
+        gather(2 * across + c)
+    g_src[...] = acc[...].astype(jnp.bfloat16).reshape(2, BLOCKS, HELD, ROWS // 2)
+
+    def g_copy(p, c):
+        to = lax.rem(b + p, BLOCKS)
+        hand = lax.rem(core + c, 2)
+        return remote(
+            g_src.at[hand, to], g_out.at[core, b], g_send.at[c, p], g_recv.at[c, p], to, 2 * chip + hand
+        )
+
+    each(1, BLOCKS, lambda p: g_copy(p, 0).start())
+    each(0, BLOCKS, lambda p: g_copy(p, 1).start())
+    own_g = pltpu.make_async_copy(g_src.at[core, b], g_out.at[core, b], local_sem.at[3])
+    own_g.start()
+
+    each(1, BLOCKS, lambda p: early_copy(p).wait())
+    own_early.wait()
+    each(1, BLOCKS, lambda p: g_copy(p, 0).wait())
+    each(0, BLOCKS, lambda p: g_copy(p, 1).wait())
+    own_g.wait()
+    for c in range(2):
+        for way in range(2):
+            far_copy(way, c).wait_send()
+            for part in range(2):
+                side_copy(way, part, c).wait_send()
+
+
+def front(x, h, gate, out_grad, out_weight):
+    half = ROWS // 2
+    dma = pltpu.SemaphoreType.DMA
+    vmem, hbm = pl.BlockSpec(memory_space=pltpu.VMEM), pl.BlockSpec(memory_space=pl.ANY)
+    bf16 = jnp.bfloat16
+    return pl.pallas_call(
+        front_kernel,
+        out_shape=(
+            jax.ShapeDtypeStruct((BLOCKS, 3, HELD, ROWS), bf16),
+            jax.ShapeDtypeStruct((2, BLOCKS, HELD, half), bf16),
+        ),
+        in_specs=[vmem, vmem, vmem, hbm, hbm],
+        out_specs=(vmem, vmem),
+        scratch_shapes=[
+            pltpu.VMEM((2, BLOCKS * HELD, 8 * ROWS), bf16),
+            pltpu.VMEM((8, 2, half // 2, ROWS), bf16),
+            pltpu.VMEM((2 * BLOCKS * HELD, half), jnp.float32),
+            pltpu.VMEM((BLOCKS, 3, HELD, ROWS), bf16),
+            pltpu.VMEM((2, BLOCKS, HELD, half), bf16),
+            dma((4,)), dma((2,)), dma((2,)), dma((2, 2, 2)), dma((2, 2, 2)), dma((2, 2)), dma((2, 2)),
+            dma((BLOCKS,)), dma((BLOCKS,)), dma((2, BLOCKS)), dma((2, BLOCKS)),
+        ],
+        compiler_params=pltpu.CompilerParams(
+            collective_id=0, has_side_effects=True, vmem_limit_bytes=48 << 20
+        ),
+    )(x, h, gate, out_grad.reshape(2, 2, half // 2, ROWS), out_weight)
+
+
+def tail_kernel(
+    done_ref, target_ref, gate_out, filter_out, rows_out, came, outbox, local_sem, done_send, done_recv, box_send, box_recv
+):
+    b = lax.axis_index("bins")
+    k = lax.axis_index("chan")
+    send_rows = 2 * ROWS // BLOCKS
+    barrier = pltpu.get_barrier_semaphore()
+
+    def greet(p):
+        pl.semaphore_signal(
+            barrier, inc=1, device_id=(lax.rem(b + p, BLOCKS), k), device_id_type=pl.DeviceIdType.MESH
+        )
+
+    each(1, BLOCKS, greet)
+    pl.semaphore_wait(barrier, BLOCKS - 1)
+
+    def done_copy(n, p):
+        to = lax.rem(b + p, BLOCKS)
+        return remote(done_ref.at[n, to], came.at[n, b], done_send.at[n, p], done_recv.at[n, p], to, k)
+
+    own_done = [pltpu.make_async_copy(done_ref.at[n, b], came.at[n, b], local_sem.at[n]) for n in range(3)]
+    for n in range(3):
+        each(1, BLOCKS, lambda p, n=n: done_copy(n, p).start())
+        own_done[n].start()
+    places = lax.broadcasted_iota(jnp.int32, (BLOCKS * send_rows, ROWS), 0)
+    chosen = jnp.where(places == target_ref[...], 1.0, 0.0).astype(jnp.bfloat16)
+
+    def arrived(n):
+        each(1, BLOCKS, lambda p: done_copy(n, p).wait())
+        own_done[n].wait()
+        return came[n].reshape(BLOCKS * HELD, ROWS)
+
+    box = lax.dot_general(
+        chosen, arrived(0), (((1,), (1,)), ((), ())), preferred_element_type=jnp.float32
+    ).astype(jnp.bfloat16)
+    outbox[...] = box.reshape(BLOCKS, send_rows, BLOCKS * HELD)
+
+    def box_copy(p):
+        to = lax.rem(b + p, BLOCKS)
+        return remote(outbox.at[to], rows_out.at[b], box_send.at[p], box_recv.at[p], to, k)
+
+    each(1, BLOCKS, lambda p: box_copy(p).start())
+    own_box = pltpu.make_async_copy(outbox.at[b], rows_out.at[b], local_sem.at[3])
+    own_box.start()
+    gate_out[...] = arrived(2).T
+    filter_out[...] = arrived(1).T.astype(jnp.float32)
+    each(1, BLOCKS, lambda p: box_copy(p).wait())
+    own_box.wait()
+
+
+def tail(done, targets):
+    dma = pltpu.SemaphoreType.DMA
+    vmem = pl.BlockSpec(memory_space=pltpu.VMEM)
+    bf16 = jnp.bfloat16
+    channels, send_rows = BLOCKS * HELD, 2 * ROWS // BLOCKS
+    return pl.pallas_call(
+        tail_kernel,
+        out_shape=(
+            jax.ShapeDtypeStruct((ROWS, channels), bf16),
+            jax.ShapeDtypeStruct((ROWS, channels), jnp.float32),
+            jax.ShapeDtypeStruct((BLOCKS, send_rows, channels), bf16),
+        ),
+        in_specs=[vmem, vmem],
+        out_specs=(vmem, vmem, vmem),
+        scratch_shapes=[
+            pltpu.VMEM((3, BLOCKS, HELD, ROWS), bf16),
+            pltpu.VMEM((BLOCKS, send_rows, channels), bf16),
+            dma((4,)), dma((3, BLOCKS)), dma((3, BLOCKS)), dma((BLOCKS,)), dma((BLOCKS,)),
+        ],
+        compiler_params=pltpu.CompilerParams(
+            collective_id=1, has_side_effects=True, vmem_limit_bytes=48 << 20
+        ),
+    )(done, targets)
 
 
 def shards(tokens_in, filters, gate, skip, out_grad, out_weight, owner, slot):
     my_index = lax.axis_index("bins")
     channels = tokens_in.shape[1]
-
-    def spread(value):
-        return lax.all_to_all(value, "bins", split_axis=0, concat_axis=0, tiled=True)
-
-    early = jnp.stack([v.T.reshape(BLOCKS, HELD, ROWS) for v in (tokens_in, filters, gate)], axis=1)
-    early = spread(early)
-    upstream = lax.dot_general(
-        out_weight,
-        lax.all_gather(out_grad, "chan", axis=1, tiled=True),
-        (((1,), (1,)), ((), ())),
-        preferred_element_type=jnp.float32,
-    ).astype(jnp.bfloat16)
-    g = spread(upstream.reshape(BLOCKS, HELD, ROWS)).reshape(BLOCKS * HELD, ROWS)
-    x, h, gates = (early[:, n].reshape(BLOCKS * HELD, ROWS) for n in range(3))
+    send_rows = 2 * ROWS // BLOCKS
+    early, g = front(tokens_in, filters, gate, out_grad, out_weight)
     own_skip = jnp.tile(lax.dynamic_slice_in_dim(skip, my_index * HELD, HELD), BLOCKS)[:, None]
-    done = transform(x, h, gates, g, own_skip)
-    done = spread(done.reshape(3, BLOCKS, HELD, ROWS).transpose(1, 0, 2, 3))
-    gate_grad, token_grad, filter_grad = (done[:, n].reshape(channels, ROWS) for n in range(3))
-    gate_grad = gate_grad.T.reshape(BLOCKS, ROWS // BLOCKS, channels)
-    filter_grad = filter_grad.T.reshape(BLOCKS, ROWS // BLOCKS, channels).astype(jnp.float32)
-    send_rows = 2 * ROWS // BLOCKS
+    done = transform(early, g, own_skip)
     targets = owner.reshape(1, -1) * send_rows + slot.reshape(1, -1) - my_index * send_rows
-    places = lax.broadcasted_iota(jnp.int32, (BLOCKS * send_rows, ROWS), 0)
-    chosen = (places == targets).astype(jnp.bfloat16)
-    outbox = lax.dot_general(
-        chosen, token_grad, (((1,), (1,)), ((), ())), preferred_element_type=jnp.float32
-    ).astype(jnp.bfloat16)
-    inbox = spread(outbox.reshape(BLOCKS, send_rows, channels))
-    return (gate_grad, filter_grad, inbox.reshape(BLOCKS * send_rows, channels))
+    gate_grad, filter_grad, grad_rows = tail(done, targets)
+    grid = (BLOCKS, ROWS // BLOCKS, channels)
+    return (gate_grad.reshape(grid), filter_grad.reshape(grid), grad_rows.reshape(BLOCKS * send_rows, channels))
 
 
 def solution(mesh):

time: 118 us -> 72.7 us (0.62)
  the two profiles are of different devices: /device:TPU:0 before, /device:TPU:1 now
where the time goes in v2:
time: 72.7 us; the launch traced here: 72 us
  Pallas kernels  61.8 us (85%)
  local copies, waits for them, and re-layouts  8.73 us (12%)
  between operations  0.75 us (1%)
    pallas_call x1, Pallas kernels, front(): pl.pallas_call(front_kernel, out_shape=(jax.ShapeDtypeStruct((BLOCKS, 3,...  35.8 us
    pallas_call x1, Pallas kernels, tail(): pl.pallas_call(tail_kernel, out_shape=(jax.ShapeDtypeStruct((ROWS, channe...  19.9 us
    unnamed x25, local copies, waits for them, and re-layouts  7.79 us
    pallas_call x1, Pallas kernels, transform(): pl.pallas_call(transform_kernel, out_shape=jax.ShapeDtypeStruct((3, BLOCK...  6.12 us

profile of v2, /device:TPU:1, one launch (start us, length us, event | category | flops | bytes accessed | tf_op | source)
XLA Modules:
  0.0 72.0 jit_solution(7310084275671029891)
XLA Ops:
  0.6 0.0 copy-start.9
  0.6 0.0 copy-start.10
  0.7 0.8 %dynamic_slice.3 = f32[16]{0:T(128)S(1)} dynamic-slice(f32[256]{0:T(256)} %param.17, s32[]{:T(128)S(6)} %select_n.3), dynamic_slice_sizes={16} | dynamic-slice | bytes 132 | tf_op jit(solution)/shard_map/dynamic_slice | solution.py:380
  1.4 0.7 add_subtract_fusion
  2.1 0.1 sub.10.target_ref
  2.2 0.1 broadcast_in_dim_tile.4.skip_ref
  2.3 0.0 copy-start
  2.3 1.6 %copy-done = bf16[256,4096]{1,0:T(8,128)(2,1)S(1)} copy-done((bf16[256,4096]{1,0:T(8,128)(2,1)S(1)}, bf16[256,4096]{1,0:T(8,128)(2,1)}, u32[]{:S(2)}) %copy-start) | copy-done | bytes 2097176
  3.9 0.0 copy-start.1
  3.9 1.0 %copy-done.1 = bf16[512,512]{1,0:T(8,128)(2,1)S(1)} copy-done((bf16[512,512]{1,0:T(8,128)(2,1)S(1)}, bf16[512,512]{1,0:T(8,128)(2,1)}, u32[]{:S(2)}) %copy-start.1) | copy-done | bytes 524312
  5.0 0.0 copy-start.5
  5.0 0.9 %copy-done.5 = bf16[512,256]{1,0:T(8,128)(2,1)S(1)} copy-done((bf16[512,256]{1,0:T(8,128)(2,1)S(1)}, bf16[512,256]{1,0:T(8,128)(2,1)}, u32[]{:S(2)}) %copy-start.5) | copy-done | bytes 262168
  5.9 0.0 copy-start.6
  5.9 0.9 %copy-done.6 = bf16[512,256]{1,0:T(8,128)(2,1)S(1)} copy-done((bf16[512,256]{1,0:T(8,128)(2,1)S(1)}, bf16[512,256]{1,0:T(8,128)(2,1)}, u32[]{:S(2)}) %copy-start.6) | copy-done | bytes 262168
  6.9 0.0 copy-start.7
  6.9 0.9 %copy-done.7 = bf16[512,256]{1,0:T(8,128)(2,1)S(1)} copy-done((bf16[512,256]{1,0:T(8,128)(2,1)S(1)}, bf16[512,256]{1,0:T(8,128)(2,1)}, u32[]{:S(2)}) %copy-start.7) | copy-done | bytes 262168
  7.8 0.0 copy-start.2
  7.8 0.0 copy-start.3
  7.8 0.0 copy-start.4
  7.8 0.0 copy-start.8
  7.8 35.8 %shard_map.157 = (bf16[16,3,16,512]{3,2,1,0:T(8,128)(2,1)S(1)}, bf16[2,16,16,256]{3,2,1,0:T(8,128)(2,1)S(1)}) custom-call(bf16[512,256]{1,0:T(8,128)(2,1)S(1)} %copy-done.5, bf16[512,256]{1,0:T(8,128)(2,1)S(1)} %copy-done.6, bf16[512,256]{1,0:T(8,128)(2,1)S(1)} %copy-done.7, bf16[2,2,128,512]{3,2,1,0:T(8,128)(2,1)S(1)} %bitcast.6, bf16[256,4096]{1,0:T(8,128)(2,1)S(1)} %copy-done), custom_call_target="tpu_custom_call" | custom-call | tf_op jit(solution)/shard_map/pallas_call | solution.py:277
  43.6 0.0 copy-done.9
  43.6 0.0 copy-done.10
  43.6 0.0 copy-done.2
  43.6 0.0 copy-done.3
  43.7 0.0 copy-done.4
  43.7 0.0 copy-done.8
  43.7 6.1 %shard_map.158.done_ref = bf16[3,16,16,512]{3,2,1,0:T(8,128)(2,1)S(1)} custom-call(bf16[16,3,16,512]{3,2,1,0:T(8,128)(2,1)S(1)} %get-tuple-element.8.early_ref, bf16[2,16,16,256]{3,2,1,0:T(8,128)(2,1)S(1)} %get-tuple-element.9.g_ref, f32[256,1]{1,0:T(8,128)S(1)} %broadcast_in_dim_tile.4.skip_ref, bf16[544,256]{1,0:T(8,128)(2,1)S(1)} %copy-done.4, ...), custom_call_target="tpu_custom_call" | custom-call | tf_op jit(solution)/shard_map/pallas_call | solution.py:122
  49.8 19.9 %shard_map.159 = (bf16[512,256]{1,0:T(8,128)(2,1)S(1)}, f32[512,256]{1,0:T(8,128)S(1)}, bf16[16,64,256]{2,1,0:T(8,128)(2,1)S(1)}) custom-call(bf16[3,16,16,512]{3,2,1,0:T(8,128)(2,1)S(1)} %shard_map.158.done_ref, s32[1,512]{1,0:T(1,128)S(1)} %sub.10.target_ref), custom_call_target="tpu_custom_call" | custom-call | tf_op jit(solution)/shard_map/pallas_call | solution.py:355
  69.7 0.7 copy.21
  70.5 0.8 %copy.22 = f32[16,32,256]{2,1,0:T(8,128)} copy(f32[16,32,256]{2,1,0:T(8,128)S(1)} %bitcast.5) | data formatting | bytes 1048576
  71.2 0.8 %copy.23 = bf16[1024,256]{1,0:T(8,128)(2,1)} copy(bf16[1024,256]{1,0:T(8,128)(2,1)S(1)} %bitcast.4) | data formatting | bytes 1048576
  (1 shorter events, 0.0 us)
Async XLA Ops:
  0.6 43.0 %copy-start.9 = (f32[17,1,512]{2,1,0:T(1,128)S(1)}, f32[17,1,512]{2,1,0:T(1,128)}, u32[]{:S(2)}) copy-start(f32[17,1,512]{2,1,0:T(1,128)} %constant.30.clone.tw_sin) | copy-start | bytes 104452
  0.6 43.0 %copy-start.10 = (f32[17,1,512]{2,1,0:T(1,128)S(1)}, f32[17,1,512]{2,1,0:T(1,128)}, u32[]{:S(2)}) copy-start(f32[17,1,512]{2,1,0:T(1,128)} %constant.29.clone.tw_cos) | copy-start | bytes 104452
  2.3 1.6 %copy-start = (bf16[256,4096]{1,0:T(8,128)(2,1)S(1)}, bf16[256,4096]{1,0:T(8,128)(2,1)}, u32[]{:S(2)}) copy-start(bf16[256,4096]{1,0:T(8,128)(2,1)} %w_hbm.1) | copy-start | bytes 6291460
  3.9 1.0 %copy-start.1 = (bf16[512,512]{1,0:T(8,128)(2,1)S(1)}, bf16[512,512]{1,0:T(8,128)(2,1)}, u32[]{:S(2)}) copy-start(bf16[512,512]{1,0:T(8,128)(2,1)} %param.18) | copy-start | bytes 1572868
  5.0 0.9 %copy-start.5 = (bf16[512,256]{1,0:T(8,128)(2,1)S(1)}, bf16[512,256]{1,0:T(8,128)(2,1)}, u32[]{:S(2)}) copy-start(bf16[512,256]{1,0:T(8,128)(2,1)} %x_ref.1) | copy-start | bytes 786436
  5.9 0.9 %copy-start.6 = (bf16[512,256]{1,0:T(8,128)(2,1)S(1)}, bf16[512,256]{1,0:T(8,128)(2,1)}, u32[]{:S(2)}) copy-start(bf16[512,256]{1,0:T(8,128)(2,1)} %h_ref.1) | copy-start | bytes 786436
  6.9 0.9 %copy-start.7 = (bf16[512,256]{1,0:T(8,128)(2,1)S(1)}, bf16[512,256]{1,0:T(8,128)(2,1)}, u32[]{:S(2)}) copy-start(bf16[512,256]{1,0:T(8,128)(2,1)} %gate_ref.1) | copy-start | bytes 786436
  7.8 35.8 %copy-start.2 = (bf16[512,512]{1,0:T(8,128)(2,1)S(1)}, bf16[512,512]{1,0:T(8,128)(2,1)}, u32[]{:S(2)}) copy-start(bf16[512,512]{1,0:T(8,128)(2,1)} %constant.32.clone.in_sin) | copy-start | bytes 1572868
  7.8 35.8 %copy-start.3 = (bf16[512,512]{1,0:T(8,128)(2,1)S(1)}, bf16[512,512]{1,0:T(8,128)(2,1)}, u32[]{:S(2)}) copy-start(bf16[512,512]{1,0:T(8,128)(2,1)} %constant.31.clone.in_cos) | copy-start | bytes 1572868
  7.8 35.8 %copy-start.4 = (bf16[544,256]{1,0:T(8,128)(2,1)S(1)}, bf16[544,256]{1,0:T(8,128)(2,1)}, u32[]{:S(2)}) copy-start(bf16[544,256]{1,0:T(8,128)(2,1)} %constant.27.clone.ahead) | copy-start | bytes 835588
  7.8 35.8 %copy-start.8 = (bf16[256,512]{1,0:T(8,128)(2,1)S(1)}, bf16[256,512]{1,0:T(8,128)(2,1)}, u32[]{:S(2)}) copy-start(bf16[256,512]{1,0:T(8,128)(2,1)} %constant.28.clone.back) | copy-start | bytes 786436

commit v3 on v2

v3 whole, which is shorter than its diff:
```python
import math

import jax
import jax.numpy as jnp
import numpy as np
from jax import lax
from jax.experimental import pallas as pl
from jax.experimental.pallas import tpu as pltpu
from jax.sharding import PartitionSpec as P

BLOCKS = 16
HELD = 16
ROWS = 512
HALF = BLOCKS + 1
LENGTH = 2 * BLOCKS * ROWS


def tables():
    k1 = np.arange(HALF)
    i = np.arange(BLOCKS)
    ang = 2.0 * np.pi * np.outer(k1, i) / (2 * BLOCKS)
    eye = np.eye(HELD)
    ahead = np.concatenate([np.kron(np.cos(ang), eye), np.kron(-np.sin(ang), eye)], axis=0)
    weight = np.where((k1 == 0) | (k1 == BLOCKS), 1.0, 2.0)[None, :] / LENGTH
    back_re = np.kron(weight * np.cos(ang).T, eye)
    back_im = np.kron(-(weight * np.sin(ang).T)[:, 1:BLOCKS], eye)
    back = np.concatenate([back_re, back_im], axis=1)
    r = np.arange(ROWS)
    twist = 2.0 * np.pi * np.outer(k1, r) / LENGTH
    inner = 2.0 * np.pi * (np.outer(r, r) % ROWS) / ROWS
    return (
        jnp.asarray(ahead, jnp.bfloat16),
        jnp.asarray(back, jnp.bfloat16),
        jnp.asarray(np.cos(twist)[:, None, :], jnp.float32),
        jnp.asarray(np.sin(twist)[:, None, :], jnp.float32),
        jnp.asarray(np.cos(inner), jnp.bfloat16),
        jnp.asarray(np.sin(inner), jnp.bfloat16),
    )


def mm(a, b):
    return jnp.dot(a, b, preferred_element_type=jnp.float32)


def stage_rows(value):
    return value.reshape(HALF, HELD, ROWS)


def flat(value):
    return value.reshape(HALF * HELD, ROWS)


def forward(value, ahead, tw_cos, tw_sin, in_cos, in_sin):
    part = mm(ahead, value)
    n = HALF * HELD
    re, im = stage_rows(part[:n]), stage_rows(part[n:])
    z_re = flat(re * tw_cos + im * tw_sin)
    z_im = flat(im * tw_cos - re * tw_sin)
    z = jnp.concatenate([z_re, z_im], axis=0).astype(jnp.bfloat16)
    by_cos, by_sin = mm(z, in_cos), mm(z, in_sin)
    return by_cos[:n] + by_sin[n:], by_cos[n:] - by_sin[:n]


def inverse(s_re, s_im, back, tw_cos, tw_sin, in_cos, in_sin):
    n = HALF * HELD
    q = jnp.concatenate([s_re, s_im], axis=0).astype(jnp.bfloat16)
    by_cos, by_sin = mm(q, in_cos), mm(q, in_sin)
    re, im = stage_rows(by_cos[:n] - by_sin[n:]), stage_rows(by_cos[n:] + by_sin[:n])
    t_re = flat(re * tw_cos - im * tw_sin)
    t_im = flat(im * tw_cos + re * tw_sin)[HELD : BLOCKS * HELD]
    t = jnp.concatenate([t_re, t_im], axis=0).astype(jnp.bfloat16)
    return mm(back, t)


def to_columns(value):
    group = lax.broadcasted_iota(jnp.int32, (HELD, 128), 1) // 32
    out = [[None] * 4 for _ in range(BLOCKS)]
    for i_hi in range(4):
        for j_hi in range(4):
            tiles = [
                value[(4 * i_hi + i_lo) * HELD : (4 * i_hi + i_lo + 1) * HELD, 128 * j_hi : 128 * (j_hi + 1)]
                for i_lo in range(4)
            ]
            for j_lo in range(4):
                acc = None
                for i_lo in range(4):
                    shift = (32 * (i_lo - j_lo)) % 128
                    turned = pltpu.roll(tiles[i_lo], shift, 1) if shift else tiles[i_lo]
                    acc = turned if acc is None else jnp.where(group == i_lo, turned, acc)
                out[4 * j_hi + j_lo][i_hi] = acc
    return jnp.concatenate([jnp.concatenate(row, axis=1) for row in out], axis=0)


def remote(src, dst, send, recv, bins, chan):
    return pltpu.make_async_remote_copy(
        src_ref=src,
        dst_ref=dst,
        send_sem=send,
        recv_sem=recv,
        device_id=(bins, chan),
        device_id_type=pl.DeviceIdType.MESH,
    )


def kernel(
    x_hbm, h_hbm, gate_hbm, skip_hbm, og_hbm, w_hbm, owner_hbm, slot_hbm, *rest
):
    tables_hbm, rest = rest[:TABLES], rest[TABLES:]
    gate_out, filter_out, rows_out = rest[:3]
    (
        raw, skip_ref, owner_ref, slot_ref, *rest
    ) = rest[3:]
    tables_ref, rest = rest[:TABLES], rest[TABLES:]
    (
        w_all, og_all, acc, early_src, early, g_src, g_came, done, came, outbox, chosen,
        local_sem, w_sem, mate_sem, side_send, side_recv, far_send, far_recv,
        early_send, early_recv, g_send, g_recv, done_send, done_recv, box_send, box_recv,
    ) = rest
    f32, bf16 = jnp.float32, jnp.bfloat16
    rows = BLOCKS * HELD
    send_rows = 2 * ROWS // BLOCKS
    b = lax.axis_index("bins")
    k = lax.axis_index("chan")
    b_y, b_z = lax.div(b, 4), lax.rem(b, 4)
    chip, core = lax.div(k, 2), lax.rem(k, 2)
    right, left, across = lax.rem(chip + 1, 4), lax.rem(chip + 3, 4), lax.rem(chip + 2, 4)
    mate = 2 * chip + 1 - core

    def peer(p):
        return 4 * lax.rem(b_y + p // 4, 4) + lax.rem(b_z + p % 4, 4)

    local = []

    def bring(src, dst):
        copy = pltpu.make_async_copy(src, dst, local_sem.at[len(local)])
        copy.start()
        local.append(copy)
        return copy

    own_raw = [bring(ref, raw.at[n]) for n, ref in enumerate((x_hbm, h_hbm, gate_hbm))]
    own_og = bring(og_hbm.at[core], og_all.at[k])
    own_w = bring(w_hbm, w_all.at[core])
    own_small = [bring(*pair) for pair in ((skip_hbm, skip_ref), (owner_hbm, owner_ref), (slot_hbm, slot_ref))]
    own_tables = [bring(*pair) for pair in zip(tables_hbm, tables_ref)]

    barrier = pltpu.get_barrier_semaphore()

    def greet(bins, chan):
        pl.semaphore_signal(barrier, inc=1, device_id=(bins, chan), device_id_type=pl.DeviceIdType.MESH)

    for p in ORDER:
        greet(peer(p), k)
        greet(peer(p), mate)
    greet(b, mate)
    for side in (right, left):
        for c in range(2):
            greet(b, 2 * side + c)
    pl.semaphore_wait(barrier, 2 * BLOCKS - 1 + 4)

    def side_copy(way, part, c):
        to = (right, left)[way]
        return remote(
            og_hbm.at[c, part], og_all.at[k, part],
            side_send.at[way, part, c], side_recv.at[way, part, core], b, 2 * to + c,
        )

    for turn in range(2):
        for c in range(2):
            side_copy(0, turn, c).start()
            side_copy(1, 1 - turn, c).start()
    mate_og = remote(og_hbm.at[1 - core], og_all.at[k], mate_sem.at[0], mate_sem.at[1], b, mate)
    mate_og.start()
    mate_w = remote(w_hbm, w_all.at[core], w_sem.at[0], w_sem.at[1], b, mate)
    mate_w.start()

    for n in range(3):
        own_raw[n].wait()
        early_src[:, n] = raw[n].T.reshape(BLOCKS, HELD, ROWS)

    def early_copy(p):
        to = peer(p)
        return remote(early_src.at[to], early.at[b], early_send.at[p], early_recv.at[p], to, k)

    for p in ORDER:
        early_copy(p).start()
    own_early = bring(early_src.at[b], early.at[b])

    def side_arrived(way, part, c):
        src = 2 * (left, right)[way] + c
        return remote(
            og_hbm.at[c, part], og_all.at[src, part],
            side_send.at[way, part, c], side_recv.at[way, part, c], b, mate,
        )

    def far_copy(way, c):
        src = 2 * (left, right)[way] + c
        to = (right, left)[way]
        return remote(
            og_all.at[src, way], og_all.at[src, way],
            far_send.at[way, c], far_recv.at[way, c], b, 2 * to + core,
        )

    for c in range(2):
        for way in range(2):
            side_arrived(way, way, c).wait_recv()
            far_copy(way, c).start()

    def gather(source, first=False):
        columns = pl.ds(pl.multiple_of(source * ROWS, ROWS), ROWS)
        weights = w_all[:, :, columns].reshape(2 * rows, ROWS)
        term = lax.dot_general(
            weights, og_all[source].reshape(ROWS // 2, ROWS), (((1,), (1,)), ((), ())), preferred_element_type=f32
        )
        acc[...] = term if first else acc[...] + term

    own_w.wait()
    own_og.wait()
    mate_w.wait()
    mate_og.wait()
    gather(k, True)
    gather(mate)
    for c in range(2):
        for way in range(2):
            side_arrived(way, 1 - way, c).wait_recv()
            gather(2 * (left, right)[way] + c)
    for copy in own_small + own_tables:
        copy.wait()
    for c in range(2):
        for way in range(2):
            far_copy(way, c).wait_recv()
        gather(2 * across + c)
    g_src[...] = acc[...].astype(bf16).reshape(2, BLOCKS, HELD, ROWS // 2)

    def g_copy(p, c):
        to = peer(p)
        hand = lax.rem(core + c, 2)
        return remote(
            g_src.at[hand, to], g_came.at[core, b], g_send.at[c, p], g_recv.at[c, p], to, 2 * chip + hand
        )

    for p in ORDER:
        g_copy(p, 0).start()
        g_copy(p, 1).start()
    g_copy(0, 1).start()
    own_g = bring(g_src.at[core, b], g_came.at[core, b])

    for p in ORDER:
        early_copy(p).wait()
    own_early.wait()
    ahead, back, tw_cos, tw_sin, in_cos, in_sin = (ref[...] for ref in tables_ref)
    forward_tables = (ahead, tw_cos, tw_sin, in_cos, in_sin)
    inverse_tables = (back, tw_cos, tw_sin, in_cos, in_sin)
    x = early[:, 0].reshape(rows, ROWS)
    x_re, x_im = forward(x, *forward_tables)
    h_re, h_im = forward(early[:, 1].reshape(rows, ROWS), *forward_tables)
    conv = inverse(x_re * h_re - x_im * h_im, x_re * h_im + x_im * h_re, *inverse_tables)
    lanes = lax.broadcasted_iota(jnp.int32, (rows, rows), 1)
    held = lax.rem(lax.broadcasted_iota(jnp.int32, (rows, rows), 0), HELD)
    skip = jnp.sum(jnp.where(lanes == held + HELD * b, skip_ref[...], 0.0), axis=1, keepdims=True)
    with_skip = conv + skip * x.astype(f32)
    target = owner_ref[...] * send_rows + slot_ref[...] - b * send_rows
    target = jnp.concatenate([target[i : i + 1] for i in range(BLOCKS)], axis=1)
    places = lax.broadcasted_iota(jnp.int32, (BLOCKS * send_rows, ROWS), 0)
    chosen[...] = jnp.where(places == target, 1.0, 0.0).astype(bf16)

    for p in ORDER:
        g_copy(p, 0).wait()
        g_copy(p, 1).wait()
    g_copy(0, 1).wait()
    own_g.wait()
    g = jnp.concatenate([g_came[0].reshape(rows, ROWS // 2), g_came[1].reshape(rows, ROWS // 2)], axis=1)
    g = g.astype(f32)
    dy = (g * early[:, 2].reshape(rows, ROWS).astype(f32)).astype(bf16)
    y_re, y_im = forward(dy, *forward_tables)

    def done_copy(n, p):
        to = peer(p)
        return remote(done.at[n, to], came.at[n, b], done_send.at[n, p], done_recv.at[n, p], to, k)

    own_done = []

    def put(n, value):
        done[n] = to_columns(value).astype(bf16).reshape(BLOCKS, HELD, ROWS)
        for p in ORDER:
            done_copy(n, p).start()
        own_done.append(bring(done.at[n, b], came.at[n, b]))

    grad = inverse(h_re * y_re + h_im * y_im, h_re * y_im - h_im * y_re, *inverse_tables)
    put(0, grad + skip * dy.astype(f32))
    lag = inverse(y_re * x_re + y_im * x_im, y_im * x_re - y_re * x_im, *inverse_tables)
    put(1, lag * (1.0 / math.sqrt(BLOCKS * ROWS)))
    put(2, g * with_skip)

    def arrived(n):
        for p in ORDER:
            done_copy(n, p).wait()
        own_done[n].wait()
        return came[n].reshape(rows, ROWS)

    box = lax.dot_general(chosen[...], arrived(0), (((1,), (1,)), ((), ())), preferred_element_type=f32)
    outbox[...] = box.astype(bf16).reshape(BLOCKS, send_rows, rows)

    def box_copy(p):
        to = peer(p)
        return remote(outbox.at[to], rows_out.at[b], box_send.at[p], box_recv.at[p], to, k)

    for p in ORDER:
        box_copy(p).start()
    own_box = bring(outbox.at[b], rows_out.at[b])
    filter_out[...] = arrived(1).T.astype(f32)
    gate_out[...] = arrived(2).T
    for c in range(2):
        for way in range(2):
            far_copy(way, c).wait_send()
            for part in range(2):
                side_copy(way, part, c).wait_send()
    for p in ORDER:
        box_copy(p).wait()
    own_box.wait()


ORDER = sorted(range(1, BLOCKS), key=lambda p: -(min(p // 4, 4 - p // 4) + min(p % 4, 4 - p % 4)))
TABLES = 6


def shards(tokens_in, filters, gate, skip, out_grad, out_weight, owner, slot):
    channels = tokens_in.shape[1]
    send_rows = 2 * ROWS // BLOCKS
    half = ROWS // 2
    dma = pltpu.SemaphoreType.DMA
    vmem, hbm = pl.BlockSpec(memory_space=pltpu.VMEM), pl.BlockSpec(memory_space=pl.ANY)
    f32, bf16 = jnp.float32, jnp.bfloat16
    constants = tables()
    operands = (
        tokens_in, filters, gate, skip.reshape(1, channels), out_grad.reshape(2, 2, half // 2, ROWS), out_weight,
        owner, slot, *constants,
    )
    gate_grad, filter_grad, grad_rows = pl.pallas_call(
        kernel,
        out_shape=(
            jax.ShapeDtypeStruct((ROWS, channels), bf16),
            jax.ShapeDtypeStruct((ROWS, channels), f32),
            jax.ShapeDtypeStruct((BLOCKS, send_rows, channels), bf16),
        ),
        in_specs=[hbm] * len(operands),
        out_specs=(vmem, vmem, vmem),
        scratch_shapes=[
            pltpu.VMEM((3, ROWS, channels), bf16),
            pltpu.VMEM((1, channels), f32),
            pltpu.VMEM(owner.shape, jnp.int32),
            pltpu.VMEM(slot.shape, jnp.int32),
            *(pltpu.VMEM(c.shape, c.dtype) for c in constants),
            pltpu.VMEM((2, channels, 8 * ROWS), bf16),
            pltpu.VMEM((8, 2, half // 2, ROWS), bf16),
            pltpu.VMEM((2 * channels, half), f32),
            pltpu.VMEM((BLOCKS, 3, HELD, ROWS), bf16),
            pltpu.VMEM((BLOCKS, 3, HELD, ROWS), bf16),
            pltpu.VMEM((2, BLOCKS, HELD, half), bf16),
            pltpu.VMEM((2, BLOCKS, HELD, half), bf16),
            pltpu.VMEM((3, BLOCKS, HELD, ROWS), bf16),
            pltpu.VMEM((3, BLOCKS, HELD, ROWS), bf16),
            pltpu.VMEM((BLOCKS, send_rows, channels), bf16),
            pltpu.VMEM((BLOCKS * send_rows, ROWS), bf16),
            dma((24,)), dma((2,)), dma((2,)), dma((2, 2, 2)), dma((2, 2, 2)), dma((2, 2)), dma((2, 2)),
            dma((BLOCKS,)), dma((BLOCKS,)), dma((2, BLOCKS)), dma((2, BLOCKS)),
            dma((3, BLOCKS)), dma((3, BLOCKS)), dma((BLOCKS,)), dma((BLOCKS,)),
        ],
        compiler_params=pltpu.CompilerParams(
            collective_id=0, has_side_effects=True, vmem_limit_bytes=67043328
        ),
    )(*operands)
    grid = (BLOCKS, ROWS // BLOCKS, channels)
    return (gate_grad.reshape(grid), filter_grad.reshape(grid), grad_rows.reshape(BLOCKS * send_rows, channels))


def solution(mesh):
    return jax.shard_map(
        shards,
        mesh=mesh,
        in_specs=(
            P("bins", "chan"),
            P("bins", "chan"),
            P("bins", "chan"),
            P("chan"),
            P("bins", "chan"),
            P("chan", None),
            P(None, "bins"),
            P(None, "bins"),
        ),
        out_specs=(P(None, "bins", "chan"), P(None, "bins", "chan"), P("bins", "chan")),
        check_vma=False,
    )
```

time: 72.7 us -> 63 us (0.87)
  Pallas kernels: 61.8 us -> 56.7 us
  local copies, waits for them, and re-layouts: 8.73 us -> 5.42 us
    pallas_call x3 -> x1, Pallas kernels: 61.8 us -> 56.7 us  [shards(): pl.pallas_call(kernel, out_shape=(jax.ShapeDtypeStruct((ROWS, channels),...]
    unnamed x25 -> x3, local copies, waits for them, and re-layouts: 7.79 us -> 5.42 us
    dynamic_slice x1 -> x0, local copies, waits for them, and re-layouts: 0.76 us -> none  [shards(): lax.dynamic_slice_in_dim(skip, my_index * HELD, HELD)]
where the time goes in v3:
time: 63 us; the launch traced here: 62.8 us
  Pallas kernels  56.7 us (90%)
  local copies, waits for them, and re-layouts  5.42 us (9%)
  between operations  0.64 us (1%)
    pallas_call x1, Pallas kernels, shards(): pl.pallas_call(kernel, out_shape=(jax.ShapeDtypeStruct((ROWS, channels),...  56.7 us
    unnamed x3, local copies, waits for them, and re-layouts  5.42 us

profile of v3, /device:TPU:1, one launch (start us, length us, event | category | flops | bytes accessed | tf_op | source)
XLA Modules:
  0.0 62.8 jit_solution(8460508786854312895)
XLA Ops:
  0.6 56.7 %shard_map.157 = (bf16[512,256]{1,0:T(8,128)(2,1)}, f32[512,256]{1,0:T(8,128)}, bf16[16,64,256]{2,1,0:T(8,128)(2,1)}) custom-call(bf16[512,256]{1,0:T(8,128)(2,1)} %x_hbm.1, bf16[512,256]{1,0:T(8,128)(2,1)} %h_hbm.1, bf16[512,256]{1,0:T(8,128)(2,1)} %gate_hbm.1, f32[1,256]{1,0:T(1,128)} %bitcast.9, bf16[2,2,128,512]{3,2,1,0:T(8,128)(2,1)} %bitcast.5, ...), custom_call_target="tpu_custom_call" | custom-call | tf_op jit(solution)/shard_map/pallas_call | solution.py:338
  57.4 1.7 %copy.20 = bf16[16,32,256]{2,1,0:T(8,128)(2,1)} copy(bf16[16,32,256]{2,1,0:T(8,128)(2,1)} %bitcast.8) | data formatting | bytes 524288
  59.0 1.9 %copy.21 = f32[16,32,256]{2,1,0:T(8,128)} copy(f32[16,32,256]{2,1,0:T(8,128)} %bitcast.7) | data formatting | bytes 1048576
  60.9 1.9 %copy.22 = bf16[1024,256]{1,0:T(8,128)(2,1)} copy(bf16[1024,256]{1,0:T(8,128)(2,1)} %bitcast.6) | data formatting | bytes 1048576

commit v4 on v3

--- a/solution.py
+++ b/solution.py
@@ -112,7 +112,7 @@
     ) = rest[3:]
     tables_ref, rest = rest[:TABLES], rest[TABLES:]
     (
-        w_all, og_all, acc, early_src, early, g_src, g_came, done, came, outbox, chosen,
+        w_all, og_all, acc, early_src, early, g_src, g_came, done, came, outbox, chosen, turned,
         local_sem, w_sem, mate_sem, side_send, side_recv, far_send, far_recv,
         early_send, early_recv, g_send, g_recv, done_send, done_recv, box_send, box_recv,
     ) = rest
@@ -225,25 +225,6 @@
             gather(2 * (left, right)[way] + c)
     for copy in own_small + own_tables:
         copy.wait()
-    for c in range(2):
-        for way in range(2):
-            far_copy(way, c).wait_recv()
-        gather(2 * across + c)
-    g_src[...] = acc[...].astype(bf16).reshape(2, BLOCKS, HELD, ROWS // 2)
-
-    def g_copy(p, c):
-        to = peer(p)
-        hand = lax.rem(core + c, 2)
-        return remote(
-            g_src.at[hand, to], g_came.at[core, b], g_send.at[c, p], g_recv.at[c, p], to, 2 * chip + hand
-        )
-
-    for p in ORDER:
-        g_copy(p, 0).start()
-        g_copy(p, 1).start()
-    g_copy(0, 1).start()
-    own_g = bring(g_src.at[core, b], g_came.at[core, b])
-
     for p in ORDER:
         early_copy(p).wait()
     own_early.wait()
@@ -263,6 +244,25 @@
     places = lax.broadcasted_iota(jnp.int32, (BLOCKS * send_rows, ROWS), 0)
     chosen[...] = jnp.where(places == target, 1.0, 0.0).astype(bf16)
 
+    for c in range(2):
+        for way in range(2):
+            far_copy(way, c).wait_recv()
+        gather(2 * across + c)
+    g_src[...] = acc[...].astype(bf16).reshape(2, BLOCKS, HELD, ROWS // 2)
+
+    def g_copy(p, c):
+        to = peer(p)
+        hand = lax.rem(core + c, 2)
+        return remote(
+            g_src.at[hand, to], g_came.at[core, b], g_send.at[c, p], g_recv.at[c, p], to, 2 * chip + hand
+        )
+
+    for p in ORDER:
+        g_copy(p, 0).start()
+        g_copy(p, 1).start()
+    g_copy(0, 1).start()
+    own_g = bring(g_src.at[core, b], g_came.at[core, b])
+
     for p in ORDER:
         g_copy(p, 0).wait()
         g_copy(p, 1).wait()
@@ -270,26 +270,26 @@
     own_g.wait()
     g = jnp.concatenate([g_came[0].reshape(rows, ROWS // 2), g_came[1].reshape(rows, ROWS // 2)], axis=1)
     g = g.astype(f32)
-    dy = (g * early[:, 2].reshape(rows, ROWS).astype(f32)).astype(bf16)
-    y_re, y_im = forward(dy, *forward_tables)
-
     def done_copy(n, p):
         to = peer(p)
         return remote(done.at[n, to], came.at[n, b], done_send.at[n, p], done_recv.at[n, p], to, k)
 
-    own_done = []
+    own_done = {}
 
     def put(n, value):
         done[n] = to_columns(value).astype(bf16).reshape(BLOCKS, HELD, ROWS)
         for p in ORDER:
             done_copy(n, p).start()
-        own_done.append(bring(done.at[n, b], came.at[n, b]))
+        own_done[n] = bring(done.at[n, b], came.at[n, b])
+
+    put(2, g * with_skip)
+    dy = (g * early[:, 2].reshape(rows, ROWS).astype(f32)).astype(bf16)
+    y_re, y_im = forward(dy, *forward_tables)
 
     grad = inverse(h_re * y_re + h_im * y_im, h_re * y_im - h_im * y_re, *inverse_tables)
     put(0, grad + skip * dy.astype(f32))
     lag = inverse(y_re * x_re + y_im * x_im, y_im * x_re - y_re * x_im, *inverse_tables)
     put(1, lag * (1.0 / math.sqrt(BLOCKS * ROWS)))
-    put(2, g * with_skip)
 
     def arrived(n):
         for p in ORDER:
@@ -307,8 +307,10 @@
     for p in ORDER:
         box_copy(p).start()
     own_box = bring(outbox.at[b], rows_out.at[b])
-    filter_out[...] = arrived(1).T.astype(f32)
-    gate_out[...] = arrived(2).T
+    results = []
+    for n, out in ((2, gate_out), (1, filter_out)):
+        turned[n - 1] = arrived(n).T
+        results.append(bring(turned.at[n - 1], out))
     for c in range(2):
         for way in range(2):
             far_copy(way, c).wait_send()
@@ -317,10 +319,58 @@
     for p in ORDER:
         box_copy(p).wait()
     own_box.wait()
+    for copy in results:
+        copy.wait()
 
 
 ORDER = sorted(range(1, BLOCKS), key=lambda p: -(min(p // 4, 4 - p // 4) + min(p % 4, 4 - p % 4)))
 TABLES = 6
+
+
+def finish_kernel(gate_hbm, filter_hbm, rows_hbm, gate_out, filter_out, rows_out, gate, taps, wide, moved, sem):
+    pieces = 2
+    half, part = ROWS // pieces, BLOCKS // pieces
+    steps = []
+    for n in range(pieces):
+        some, blocks = pl.ds(n * half, half), pl.ds(n * part, part)
+        steps += [
+            (filter_hbm.at[some], taps.at[some], wide.at[some], filter_out.at[some], some),
+            (rows_hbm.at[blocks], moved.at[blocks], moved.at[blocks], rows_out.at[blocks], None),
+            (gate_hbm.at[some], gate.at[some], gate.at[some], gate_out.at[some], None),
+        ]
+    reads = [pltpu.make_async_copy(src, held, sem.at[0, n]) for n, (src, held, _, _, _) in enumerate(steps)]
+    writes = [pltpu.make_async_copy(held, dst, sem.at[1, n]) for n, (_, _, held, dst, _) in enumerate(steps)]
+    for read in reads:
+        read.start()
+    for read, write, step in zip(reads, writes, steps):
+        read.wait()
+        if step[4] is not None:
+            wide[step[4]] = taps[step[4]].astype(jnp.float32)
+        write.start()
+    for write in writes:
+        write.wait()
+
+
+def finish(gate_grad, filter_grad, grad_rows):
+    f32 = jnp.float32
+    return pl.pallas_call(
+        finish_kernel,
+        out_shape=(
+            jax.ShapeDtypeStruct(gate_grad.shape, gate_grad.dtype),
+            jax.ShapeDtypeStruct(filter_grad.shape, f32),
+            jax.ShapeDtypeStruct(grad_rows.shape, grad_rows.dtype),
+        ),
+        in_specs=[pl.BlockSpec(memory_space=pl.ANY)] * 3,
+        out_specs=(pl.BlockSpec(memory_space=pl.ANY),) * 3,
+        scratch_shapes=[
+            pltpu.VMEM(gate_grad.shape, gate_grad.dtype),
+            pltpu.VMEM(filter_grad.shape, filter_grad.dtype),
+            pltpu.VMEM(filter_grad.shape, f32),
+            pltpu.VMEM(grad_rows.shape, grad_rows.dtype),
+            pltpu.SemaphoreType.DMA((2, 6)),
+        ],
+        compiler_params=pltpu.CompilerParams(vmem_limit_bytes=67043328),
+    )(gate_grad, filter_grad, grad_rows)
 
 
 def shards(tokens_in, filters, gate, skip, out_grad, out_weight, owner, slot):
@@ -328,7 +378,7 @@
     send_rows = 2 * ROWS // BLOCKS
     half = ROWS // 2
     dma = pltpu.SemaphoreType.DMA
-    vmem, hbm = pl.BlockSpec(memory_space=pltpu.VMEM), pl.BlockSpec(memory_space=pl.ANY)
+    hbm = pl.BlockSpec(memory_space=pl.ANY)
     f32, bf16 = jnp.float32, jnp.bfloat16
     constants = tables()
     operands = (
@@ -339,11 +389,11 @@
         kernel,
         out_shape=(
             jax.ShapeDtypeStruct((ROWS, channels), bf16),
-            jax.ShapeDtypeStruct((ROWS, channels), f32),
+            jax.ShapeDtypeStruct((ROWS, channels), bf16),
             jax.ShapeDtypeStruct((BLOCKS, send_rows, channels), bf16),
         ),
         in_specs=[hbm] * len(operands),
-        out_specs=(vmem, vmem, vmem),
+        out_specs=(hbm, hbm, hbm),
         scratch_shapes=[
             pltpu.VMEM((3, ROWS, channels), bf16),
             pltpu.VMEM((1, channels), f32),
@@ -361,6 +411,7 @@
             pltpu.VMEM((3, BLOCKS, HELD, ROWS), bf16),
             pltpu.VMEM((BLOCKS, send_rows, channels), bf16),
             pltpu.VMEM((BLOCKS * send_rows, ROWS), bf16),
+            pltpu.VMEM((2, ROWS, channels), bf16),
             dma((24,)), dma((2,)), dma((2,)), dma((2, 2, 2)), dma((2, 2, 2)), dma((2, 2)), dma((2, 2)),
             dma((BLOCKS,)), dma((BLOCKS,)), dma((2, BLOCKS)), dma((2, BLOCKS)),
             dma((3, BLOCKS)), dma((3, BLOCKS)), dma((BLOCKS,)), dma((BLOCKS,)),
@@ -369,6 +420,7 @@
             collective_id=0, has_side_effects=True, vmem_limit_bytes=67043328
         ),
     )(*operands)
+    gate_grad, filter_grad, grad_rows = finish(gate_grad, filter_grad, grad_rows)
     grid = (BLOCKS, ROWS // BLOCKS, channels)
     return (gate_grad.reshape(grid), filter_grad.reshape(grid), grad_rows.reshape(BLOCKS * send_rows, channels))
 

time: 63 us -> 57.4 us (0.911)
  local copies, waits for them, and re-layouts: 5.42 us -> 0 us
    unnamed x3 -> x0, local copies, waits for them, and re-layouts: 5.42 us -> none
    pallas_call x1, Pallas kernels: 56.7 us -> 54.2 us  [shards(): pl.pallas_call(kernel, out_shape=(jax.ShapeDtypeStruct((ROWS, channels),...]
    pallas_call x0 -> x1, Pallas kernels: none -> 2.08 us  [finish(): pl.pallas_call(finish_kernel, out_shape=(jax.ShapeDtypeStruct(gate_grad.s...]
where the time goes in v4:
time: 57.4 us; the launch traced here: 56.9 us
  Pallas kernels  56.2 us (98%)
  between operations  0.64 us (1%)
    pallas_call x1, Pallas kernels, shards(): pl.pallas_call(kernel, out_shape=(jax.ShapeDtypeStruct((ROWS, channels),...  54.2 us
    pallas_call x1, Pallas kernels, finish(): pl.pallas_call(finish_kernel, out_shape=(jax.ShapeDtypeStruct(gate_grad.s...  2.08 us

profile of v4, /device:TPU:1, one launch (start us, length us, event | category | flops | bytes accessed | tf_op | source)
XLA Modules:
  0.0 56.9 jit_solution(824919859802192691)
XLA Ops:
  0.6 54.2 %shard_map.157 = (bf16[512,256]{1,0:T(8,128)(2,1)}, bf16[512,256]{1,0:T(8,128)(2,1)}, bf16[16,64,256]{2,1,0:T(8,128)(2,1)}) custom-call(bf16[512,256]{1,0:T(8,128)(2,1)} %x_hbm.1, bf16[512,256]{1,0:T(8,128)(2,1)} %h_hbm.1, bf16[512,256]{1,0:T(8,128)(2,1)} %gate_hbm.1, f32[1,256]{1,0:T(1,128)} %bitcast.6, bf16[2,2,128,512]{3,2,1,0:T(8,128)(2,1)} %bitcast.5, ...), custom_call_target="tpu_custom_call" | custom-call | tf_op jit(solution)/shard_map/pallas_call | solution.py:388
  54.8 2.1 %shard_map.158 = (bf16[512,256]{1,0:T(8,128)(2,1)}, f32[512,256]{1,0:T(8,128)}, bf16[16,64,256]{2,1,0:T(8,128)(2,1)}) custom-call(bf16[512,256]{1,0:T(8,128)(2,1)} %get-tuple-element.9.gate_hbm, bf16[512,256]{1,0:T(8,128)(2,1)} %get-tuple-element.10.filter_hbm, bf16[16,64,256]{2,1,0:T(8,128)(2,1)} %get-tuple-element.11.rows_hbm), custom_call_target="tpu_custom_call" | custom-call | tf_op jit(solution)/shard_map/pallas_call | solution.py:356

commit v5 on v4

--- a/solution.py
+++ b/solution.py
@@ -112,9 +112,9 @@
     ) = rest[3:]
     tables_ref, rest = rest[:TABLES], rest[TABLES:]
     (
-        w_all, og_all, acc, early_src, early, g_src, g_came, done, came, outbox, chosen, turned,
+        w_all, og_all, acc, early_src, early, g_src, g_came, done, came, outbox, map_src, maps, turned,
         local_sem, w_sem, mate_sem, side_send, side_recv, far_send, far_recv,
-        early_send, early_recv, g_send, g_recv, done_send, done_recv, box_send, box_recv,
+        early_send, early_recv, g_send, g_recv, done_send, done_recv, box_send, box_recv, map_send, map_recv,
     ) = rest
     f32, bf16 = jnp.float32, jnp.bfloat16
     rows = BLOCKS * HELD
@@ -239,11 +239,27 @@
     held = lax.rem(lax.broadcasted_iota(jnp.int32, (rows, rows), 0), HELD)
     skip = jnp.sum(jnp.where(lanes == held + HELD * b, skip_ref[...], 0.0), axis=1, keepdims=True)
     with_skip = conv + skip * x.astype(f32)
-    target = owner_ref[...] * send_rows + slot_ref[...] - b * send_rows
+    odd = lax.rem(b, 2)
+    target = (owner_ref[...] + odd * (1 - 2 * lax.rem(owner_ref[...], 2))) * send_rows + slot_ref[...] - b * send_rows
     target = jnp.concatenate([target[i : i + 1] for i in range(BLOCKS)], axis=1)
     places = lax.broadcasted_iota(jnp.int32, (BLOCKS * send_rows, ROWS), 0)
-    chosen[...] = jnp.where(places == target, 1.0, 0.0).astype(bf16)
-
+    chosen = jnp.where(places == target, 1.0, 0.0).astype(bf16)
+    token = lax.broadcasted_iota(jnp.int32, (16, ROWS), 1)
+    which = lax.broadcasted_iota(jnp.int32, (16, ROWS), 0)
+    digits = jnp.where(which == 0, lax.rem(token, 128), jnp.where(which == 1, lax.div(token, 128) + 1, 0))
+    digits = lax.dot_general(
+        digits.astype(f32).astype(bf16), chosen, (((1,), (1,)), ((), ())), preferred_element_type=f32
+    )
+    origin = (digits[0:1] + 128.0 * digits[1:2]).astype(jnp.int32)
+    map_src[...] = jnp.concatenate([origin[:, 128 * n : 128 * (n + 1)] for n in range(8)], axis=0)
+
+    def map_copy(p):
+        to = peer(p)
+        return remote(map_src, maps.at[b], map_send.at[p], map_recv.at[p], to, k)
+
+    for p in ORDER:
+        map_copy(p).start()
+    own_map = bring(map_src, maps.at[b])
     for c in range(2):
         for way in range(2):
             far_copy(way, c).wait_recv()
@@ -282,14 +298,45 @@
             done_copy(n, p).start()
         own_done[n] = bring(done.at[n, b], came.at[n, b])
 
-    put(2, g * with_skip)
+    put(0, g * with_skip)
     dy = (g * early[:, 2].reshape(rows, ROWS).astype(f32)).astype(bf16)
     y_re, y_im = forward(dy, *forward_tables)
 
-    grad = inverse(h_re * y_re + h_im * y_im, h_re * y_im - h_im * y_re, *inverse_tables)
-    put(0, grad + skip * dy.astype(f32))
     lag = inverse(y_re * x_re + y_im * x_im, y_im * x_re - y_re * x_im, *inverse_tables)
     put(1, lag * (1.0 / math.sqrt(BLOCKS * ROWS)))
+    grad = inverse(h_re * y_re + h_im * y_im, h_re * y_im - h_im * y_re, *inverse_tables)
+    columns = to_columns(grad + skip * dy.astype(f32))
+    for p in ORDER:
+        map_copy(p).wait()
+    own_map.wait()
+    low_half = lax.broadcasted_iota(jnp.int32, (HELD, 128), 1) < 64
+    for m in range(BLOCKS // 2):
+        picked = []
+        for j in (2 * m, 2 * m + 1):
+            held = columns[j * HELD : (j + 1) * HELD]
+            lane, tile = lax.rem(maps[j], 128), lax.div(maps[j], 128)
+            tiles = []
+            for n in range(8):
+                at = jnp.broadcast_to(lane[n : n + 1], (HELD, 128))
+                which = jnp.broadcast_to(tile[n : n + 1], (HELD, 128))
+                value = jnp.zeros((HELD, 128), f32)
+                for t in range(4):
+                    found = jnp.take_along_axis(held[:, 128 * t : 128 * (t + 1)], at, axis=1)
+                    value = jnp.where(which == t + 1, found, value)
+                tiles.append(value)
+            picked.append(tiles)
+        for n in range(8):
+            even, other = picked[0][n], picked[1][n]
+            outbox[2 * n, :, 128 * m : 128 * (m + 1)] = jnp.where(low_half, even, other).astype(bf16)
+            outbox[2 * n + 1, :, 128 * m : 128 * (m + 1)] = jnp.where(low_half, other, even).astype(bf16)
+
+    def box_copy(p):
+        to = peer(p)
+        return remote(outbox.at[to], rows_out.at[b], box_send.at[p], box_recv.at[p], to, k)
+
+    for p in ORDER:
+        box_copy(p).start()
+    own_box = bring(outbox.at[b], rows_out.at[b])
 
     def arrived(n):
         for p in ORDER:
@@ -297,20 +344,10 @@
         own_done[n].wait()
         return came[n].reshape(rows, ROWS)
 
-    box = lax.dot_general(chosen[...], arrived(0), (((1,), (1,)), ((), ())), preferred_element_type=f32)
-    outbox[...] = box.astype(bf16).reshape(BLOCKS, send_rows, rows)
-
-    def box_copy(p):
-        to = peer(p)
-        return remote(outbox.at[to], rows_out.at[b], box_send.at[p], box_recv.at[p], to, k)
-
-    for p in ORDER:
-        box_copy(p).start()
-    own_box = bring(outbox.at[b], rows_out.at[b])
     results = []
-    for n, out in ((2, gate_out), (1, filter_out)):
-        turned[n - 1] = arrived(n).T
-        results.append(bring(turned.at[n - 1], out))
+    for n, out in enumerate((gate_out, filter_out)):
+        turned[n] = arrived(n).T
+        results.append(bring(turned.at[n], out))
     for c in range(2):
         for way in range(2):
             far_copy(way, c).wait_send()
@@ -327,38 +364,49 @@
 TABLES = 6
 
 
-def finish_kernel(gate_hbm, filter_hbm, rows_hbm, gate_out, filter_out, rows_out, gate, taps, wide, moved, sem):
-    pieces = 2
-    half, part = ROWS // pieces, BLOCKS // pieces
-    steps = []
-    for n in range(pieces):
-        some, blocks = pl.ds(n * half, half), pl.ds(n * part, part)
-        steps += [
-            (filter_hbm.at[some], taps.at[some], wide.at[some], filter_out.at[some], some),
-            (rows_hbm.at[blocks], moved.at[blocks], moved.at[blocks], rows_out.at[blocks], None),
-            (gate_hbm.at[some], gate.at[some], gate.at[some], gate_out.at[some], None),
-        ]
-    reads = [pltpu.make_async_copy(src, held, sem.at[0, n]) for n, (src, held, _, _, _) in enumerate(steps)]
-    writes = [pltpu.make_async_copy(held, dst, sem.at[1, n]) for n, (_, _, held, dst, _) in enumerate(steps)]
-    for read in reads:
-        read.start()
-    for read, write, step in zip(reads, writes, steps):
-        read.wait()
-        if step[4] is not None:
-            wide[step[4]] = taps[step[4]].astype(jnp.float32)
-        write.start()
-    for write in writes:
-        write.wait()
+def finish_kernel(gate_hbm, filter_hbm, rows_hbm, gate_out, filter_out, rows_out, gate, taps, wide, moved, ranked, sem):
+    odd = lax.rem(lax.axis_index("bins"), 2)
+    span = 256
+    parts = rows_hbm.shape[1] // span
+    reads, writes = [], []
+
+    def read(src, held):
+        reads.append(pltpu.make_async_copy(src, held, sem.at[len(reads)]))
+        reads[-1].start()
+        return reads[-1]
+
+    def write(held, dst):
+        writes.append(pltpu.make_async_copy(held, dst, sem.at[8 + len(writes)]))
+        writes[-1].start()
+
+    taps_in = read(filter_hbm, taps)
+    rows_in = [read(rows_hbm.at[:, pl.ds(n * span, span)], moved.at[n]) for n in range(parts)]
+    gate_in = read(gate_hbm, gate)
+    taps_in.wait()
+    wide[...] = taps[...].astype(jnp.float32)
+    write(wide, filter_out)
+    for n in range(parts):
+        rows_in[n].wait()
+        ranked[n] = moved[n].T.reshape(span // 64, 64, 256)
+        for q in range(span // 64):
+            group = n * (span // 64) + q
+            group = group + odd * (1 - 2 * (q % 2))
+            write(ranked.at[n, q], rows_out.at[pl.ds(group * 64, 64)])
+    gate_in.wait()
+    write(gate, gate_out)
+    for copy in writes:
+        copy.wait()
 
 
 def finish(gate_grad, filter_grad, grad_rows):
     f32 = jnp.float32
+    channels, count = grad_rows.shape
     return pl.pallas_call(
         finish_kernel,
         out_shape=(
             jax.ShapeDtypeStruct(gate_grad.shape, gate_grad.dtype),
             jax.ShapeDtypeStruct(filter_grad.shape, f32),
-            jax.ShapeDtypeStruct(grad_rows.shape, grad_rows.dtype),
+            jax.ShapeDtypeStruct((count, channels), grad_rows.dtype),
         ),
         in_specs=[pl.BlockSpec(memory_space=pl.ANY)] * 3,
         out_specs=(pl.BlockSpec(memory_space=pl.ANY),) * 3,
@@ -366,8 +414,9 @@
             pltpu.VMEM(gate_grad.shape, gate_grad.dtype),
             pltpu.VMEM(filter_grad.shape, filter_grad.dtype),
             pltpu.VMEM(filter_grad.shape, f32),
-            pltpu.VMEM(grad_rows.shape, grad_rows.dtype),
-            pltpu.SemaphoreType.DMA((2, 6)),
+            pltpu.VMEM((count // 256, channels, 256), grad_rows.dtype),
+            pltpu.VMEM((count // 256, 4, 64, channels), grad_rows.dtype),
+            pltpu.SemaphoreType.DMA((32,)),
         ],
         compiler_params=pltpu.CompilerParams(vmem_limit_bytes=67043328),
     )(gate_grad, filter_grad, grad_rows)
@@ -390,7 +439,7 @@
         out_shape=(
             jax.ShapeDtypeStruct((ROWS, channels), bf16),
             jax.ShapeDtypeStruct((ROWS, channels), bf16),
-            jax.ShapeDtypeStruct((BLOCKS, send_rows, channels), bf16),
+            jax.ShapeDtypeStruct((BLOCKS, HELD, BLOCKS * send_rows), bf16),
         ),
         in_specs=[hbm] * len(operands),
         out_specs=(hbm, hbm, hbm),
@@ -407,22 +456,23 @@
             pltpu.VMEM((BLOCKS, 3, HELD, ROWS), bf16),
             pltpu.VMEM((2, BLOCKS, HELD, half), bf16),
             pltpu.VMEM((2, BLOCKS, HELD, half), bf16),
-            pltpu.VMEM((3, BLOCKS, HELD, ROWS), bf16),
-            pltpu.VMEM((3, BLOCKS, HELD, ROWS), bf16),
-            pltpu.VMEM((BLOCKS, send_rows, channels), bf16),
-            pltpu.VMEM((BLOCKS * send_rows, ROWS), bf16),
+            pltpu.VMEM((2, BLOCKS, HELD, ROWS), bf16),
+            pltpu.VMEM((2, BLOCKS, HELD, ROWS), bf16),
+            pltpu.VMEM((BLOCKS, HELD, BLOCKS * send_rows), bf16),
+            pltpu.VMEM((8, 128), jnp.int32),
+            pltpu.VMEM((BLOCKS, 8, 128), jnp.int32),
             pltpu.VMEM((2, ROWS, channels), bf16),
             dma((24,)), dma((2,)), dma((2,)), dma((2, 2, 2)), dma((2, 2, 2)), dma((2, 2)), dma((2, 2)),
             dma((BLOCKS,)), dma((BLOCKS,)), dma((2, BLOCKS)), dma((2, BLOCKS)),
-            dma((3, BLOCKS)), dma((3, BLOCKS)), dma((BLOCKS,)), dma((BLOCKS,)),
+            dma((2, BLOCKS)), dma((2, BLOCKS)), dma((BLOCKS,)), dma((BLOCKS,)), dma((BLOCKS,)), dma((BLOCKS,)),
         ],
         compiler_params=pltpu.CompilerParams(
             collective_id=0, has_side_effects=True, vmem_limit_bytes=67043328
         ),
     )(*operands)
-    gate_grad, filter_grad, grad_rows = finish(gate_grad, filter_grad, grad_rows)
+    gate_grad, filter_grad, grad_rows = finish(gate_grad, filter_grad, grad_rows.reshape(channels, -1))
     grid = (BLOCKS, ROWS // BLOCKS, channels)
-    return (gate_grad.reshape(grid), filter_grad.reshape(grid), grad_rows.reshape(BLOCKS * send_rows, channels))
+    return (gate_grad.reshape(grid), filter_grad.reshape(grid), grad_rows)
 
 
 def solution(mesh):

time: 57.4 us -> 54.9 us (0.956)
  Pallas kernels: 56.2 us -> 54.2 us
    pallas_call x1, Pallas kernels: 54.2 us -> 51.8 us  [shards(): pl.pallas_call(kernel, out_shape=(jax.ShapeDtypeStruct((ROWS, channels),...]
where the time goes in v5:
time: 54.9 us; the launch traced here: 54.8 us
  Pallas kernels  54.2 us (99%)
  between operations  0.64 us (1%)
    pallas_call x1, Pallas kernels, shards(): pl.pallas_call(kernel, out_shape=(jax.ShapeDtypeStruct((ROWS, channels),...  51.8 us
    pallas_call x1, Pallas kernels, finish(): pl.pallas_call(finish_kernel, out_shape=(jax.ShapeDtypeStruct(gate_grad.s...  2.38 us

profile of v5, /device:TPU:1, one launch (start us, length us, event | category | flops | bytes accessed | tf_op | source)
XLA Modules:
  0.0 54.8 jit_solution(6842849015174021246)
XLA Ops:
  0.6 51.8 %shard_map.157 = (bf16[512,256]{1,0:T(8,128)(2,1)}, bf16[512,256]{1,0:T(8,128)(2,1)}, bf16[16,16,1024]{2,1,0:T(8,128)(2,1)}) custom-call(bf16[512,256]{1,0:T(8,128)(2,1)} %x_hbm.1, bf16[512,256]{1,0:T(8,128)(2,1)} %h_hbm.1, bf16[512,256]{1,0:T(8,128)(2,1)} %gate_hbm.1, f32[1,256]{1,0:T(1,128)} %bitcast.7, bf16[2,2,128,512]{3,2,1,0:T(8,128)(2,1)} %bitcast.5, ...), custom_call_target="tpu_custom_call" | custom-call | tf_op jit(solution)/shard_map/pallas_call | solution.py:437
  52.4 2.4 %shard_map.158 = (bf16[512,256]{1,0:T(8,128)(2,1)}, f32[512,256]{1,0:T(8,128)}, bf16[1024,256]{1,0:T(8,128)(2,1)}) custom-call(bf16[512,256]{1,0:T(8,128)(2,1)} %get-tuple-element.9.gate_hbm, bf16[512,256]{1,0:T(8,128)(2,1)} %get-tuple-element.10.filter_hbm, bf16[256,1024]{1,0:T(8,128)(2,1)} %bitcast.6), custom_call_target="tpu_custom_call" | custom-call | tf_op jit(solution)/shard_map/pallas_call | solution.py:404

commit v6 on v5

--- a/solution.py
+++ b/solution.py
@@ -112,9 +112,11 @@
     ) = rest[3:]
     tables_ref, rest = rest[:TABLES], rest[TABLES:]
     (
-        w_all, og_all, acc, early_src, early, g_src, g_came, done, came, outbox, map_src, maps, turned,
+        w_all, og_all, acc, pair_src, pair, gate_src, gate_came, mix_src, mix, g_src, g_came, gated_src,
+        done, came, outbox, map_src, maps, turned,
         local_sem, w_sem, mate_sem, side_send, side_recv, far_send, far_recv,
-        early_send, early_recv, g_send, g_recv, done_send, done_recv, box_send, box_recv, map_send, map_recv,
+        pair_send, pair_recv, gate_send, gate_recv, mix_send, mix_recv, g_send, g_recv, gated_send, gated_recv,
+        done_send, done_recv, box_send, box_recv, map_send, map_recv,
     ) = rest
     f32, bf16 = jnp.float32, jnp.bfloat16
     rows = BLOCKS * HELD
@@ -160,7 +162,7 @@
     def side_copy(way, part, c):
         to = (right, left)[way]
         return remote(
-            og_hbm.at[c, part], og_all.at[k, part],
+            og_hbm.at[c, :, part], og_all.at[k, :, part],
             side_send.at[way, part, c], side_recv.at[way, part, core], b, 2 * to + c,
         )
 
@@ -173,72 +175,97 @@
     mate_w = remote(w_hbm, w_all.at[core], w_sem.at[0], w_sem.at[1], b, mate)
     mate_w.start()
 
-    for n in range(3):
+    for n in range(2):
         own_raw[n].wait()
-        early_src[:, n] = raw[n].T.reshape(BLOCKS, HELD, ROWS)
-
-    def early_copy(p):
-        to = peer(p)
-        return remote(early_src.at[to], early.at[b], early_send.at[p], early_recv.at[p], to, k)
-
-    for p in ORDER:
-        early_copy(p).start()
-    own_early = bring(early_src.at[b], early.at[b])
+        pair_src[:, n] = raw[n].T.reshape(BLOCKS, HELD, ROWS)
+
+    def pair_copy(p):
+        to = peer(p)
+        return remote(pair_src.at[to], pair.at[b], pair_send.at[p], pair_recv.at[p], to, k)
+
+    for p in ORDER:
+        pair_copy(p).start()
+    own_pair = bring(pair_src.at[b], pair.at[b])
+    own_raw[2].wait()
+    gate_src[...] = raw[2].T.reshape(BLOCKS, HELD, ROWS)
+
+    def gate_copy(p):
+        to = peer(p)
+        return remote(gate_src.at[to], gate_came.at[b], gate_send.at[p], gate_recv.at[p], to, k)
+
+    for p in ORDER:
+        gate_copy(p).start()
+    own_gate = bring(gate_src.at[b], gate_came.at[b])
 
     def side_arrived(way, part, c):
         src = 2 * (left, right)[way] + c
         return remote(
-            og_hbm.at[c, part], og_all.at[src, part],
+            og_hbm.at[c, :, part], og_all.at[src, :, part],
             side_send.at[way, part, c], side_recv.at[way, part, c], b, mate,
         )
 
-    def far_copy(way, c):
+    def far_copy(way, c, s):
         src = 2 * (left, right)[way] + c
         to = (right, left)[way]
         return remote(
-            og_all.at[src, way], og_all.at[src, way],
-            far_send.at[way, c], far_recv.at[way, c], b, 2 * to + core,
+            og_all.at[src, s, way], og_all.at[src, s, way],
+            far_send.at[way, c, s], far_recv.at[way, c, s], b, 2 * to + core,
         )
 
     for c in range(2):
         for way in range(2):
             side_arrived(way, way, c).wait_recv()
-            far_copy(way, c).start()
-
-    def gather(source, first=False):
+    for s in range(2):
+        for c in range(2):
+            for way in range(2):
+                far_copy(way, c, s).start()
+
+    def term(source, tokens):
         columns = pl.ds(pl.multiple_of(source * ROWS, ROWS), ROWS)
         weights = w_all[:, :, columns].reshape(2 * rows, ROWS)
-        term = lax.dot_general(
-            weights, og_all[source].reshape(ROWS // 2, ROWS), (((1,), (1,)), ((), ())), preferred_element_type=f32
-        )
-        acc[...] = term if first else acc[...] + term
+        return lax.dot_general(weights, tokens, (((1,), (1,)), ((), ())), preferred_element_type=f32)
+
+    def near(source):
+        return term(source, og_all[source].reshape(ROWS // 2, ROWS))
 
     own_w.wait()
     own_og.wait()
     mate_w.wait()
     mate_og.wait()
-    gather(k, True)
-    gather(mate)
-    for c in range(2):
-        for way in range(2):
-            side_arrived(way, 1 - way, c).wait_recv()
-            gather(2 * (left, right)[way] + c)
+    acc[...] = near(k) + near(mate)
+
     for copy in own_small + own_tables:
         copy.wait()
-    for p in ORDER:
-        early_copy(p).wait()
-    own_early.wait()
     ahead, back, tw_cos, tw_sin, in_cos, in_sin = (ref[...] for ref in tables_ref)
     forward_tables = (ahead, tw_cos, tw_sin, in_cos, in_sin)
     inverse_tables = (back, tw_cos, tw_sin, in_cos, in_sin)
-    x = early[:, 0].reshape(rows, ROWS)
-    x_re, x_im = forward(x, *forward_tables)
-    h_re, h_im = forward(early[:, 1].reshape(rows, ROWS), *forward_tables)
-    conv = inverse(x_re * h_re - x_im * h_im, x_re * h_im + x_im * h_re, *inverse_tables)
     lanes = lax.broadcasted_iota(jnp.int32, (rows, rows), 1)
     held = lax.rem(lax.broadcasted_iota(jnp.int32, (rows, rows), 0), HELD)
     skip = jnp.sum(jnp.where(lanes == held + HELD * b, skip_ref[...], 0.0), axis=1, keepdims=True)
-    with_skip = conv + skip * x.astype(f32)
+    for p in ORDER:
+        pair_copy(p).wait()
+    own_pair.wait()
+    x = pair[:, 0].reshape(rows, ROWS)
+    x_re, x_im = forward(x, *forward_tables)
+    h_re, h_im = forward(pair[:, 1].reshape(rows, ROWS), *forward_tables)
+    conv = inverse(x_re * h_re - x_im * h_im, x_re * h_im + x_im * h_re, *inverse_tables)
+    with_skip = (conv + skip * x.astype(f32)).astype(bf16)
+    for hand in range(2):
+        mix_src[hand] = with_skip[:, rows * hand : rows * (hand + 1)].reshape(BLOCKS, HELD, ROWS // 2)
+
+    def mix_copy(p, c):
+        to = peer(p)
+        hand = lax.rem(core + c, 2)
+        return remote(
+            mix_src.at[hand, to], mix.at[core, b], mix_send.at[c, p], mix_recv.at[c, p], to, 2 * chip + hand
+        )
+
+    for p in ORDER:
+        mix_copy(p, 0).start()
+        mix_copy(p, 1).start()
+    mix_copy(0, 1).start()
+    own_mix = bring(mix_src.at[core, b], mix.at[core, b])
+
     odd = lax.rem(b, 2)
     target = (owner_ref[...] + odd * (1 - 2 * lax.rem(owner_ref[...], 2))) * send_rows + slot_ref[...] - b * send_rows
     target = jnp.concatenate([target[i : i + 1] for i in range(BLOCKS)], axis=1)
@@ -260,50 +287,92 @@
     for p in ORDER:
         map_copy(p).start()
     own_map = bring(map_src, maps.at[b])
+
     for c in range(2):
         for way in range(2):
-            far_copy(way, c).wait_recv()
-        gather(2 * across + c)
-    g_src[...] = acc[...].astype(bf16).reshape(2, BLOCKS, HELD, ROWS // 2)
-
-    def g_copy(p, c):
+            side_arrived(way, 1 - way, c).wait_recv()
+            acc[...] += near(2 * (left, right)[way] + c)
+
+    def g_copy(p, c, s):
         to = peer(p)
         hand = lax.rem(core + c, 2)
         return remote(
-            g_src.at[hand, to], g_came.at[core, b], g_send.at[c, p], g_recv.at[c, p], to, 2 * chip + hand
+            g_src.at[s, hand, to], g_came.at[core, s, b],
+            g_send.at[s, c, p], g_recv.at[s, c, p], to, 2 * chip + hand,
         )
 
-    for p in ORDER:
-        g_copy(p, 0).start()
-        g_copy(p, 1).start()
-    g_copy(0, 1).start()
-    own_g = bring(g_src.at[core, b], g_came.at[core, b])
-
-    for p in ORDER:
-        g_copy(p, 0).wait()
-        g_copy(p, 1).wait()
-    g_copy(0, 1).wait()
-    own_g.wait()
-    g = jnp.concatenate([g_came[0].reshape(rows, ROWS // 2), g_came[1].reshape(rows, ROWS // 2)], axis=1)
+    own_g = []
+    for s in range(2):
+        for c in range(2):
+            for way in range(2):
+                far_copy(way, c, s).wait_recv()
+        part = acc[:, 128 * s : 128 * (s + 1)]
+        for c in range(2):
+            part = part + term(2 * across + c, og_all[2 * across + c, s].reshape(128, ROWS))
+        g_src[s] = part.astype(bf16).reshape(2, BLOCKS, HELD, 128)
+        for p in ORDER:
+            g_copy(p, 0, s).start()
+            g_copy(p, 1, s).start()
+        g_copy(0, 1, s).start()
+        own_g.append(bring(g_src.at[s, core, b], g_came.at[core, s, b]))
+
+    for p in ORDER:
+        mix_copy(p, 0).wait()
+        mix_copy(p, 1).wait()
+    mix_copy(0, 1).wait()
+    own_mix.wait()
+    g_block = jnp.concatenate([g_src[s].reshape(2 * rows, 128) for s in range(2)], axis=1).astype(f32)
+    gated = (g_block * mix[...].reshape(2 * rows, ROWS // 2).astype(f32)).astype(bf16).T
+    for hand in range(2):
+        gated_src[hand] = gated[:, rows * hand : rows * (hand + 1)].reshape(8, ROWS // BLOCKS, rows)
+
+    def gated_copy(q, c):
+        column = lax.rem(b + q, 8)
+        hand = lax.rem(core + c, 2)
+        return remote(
+            gated_src.at[hand, column], gate_out.at[b],
+            gated_send.at[c, q], gated_recv.at[b], 8 * core + column, 2 * chip + hand,
+        )
+
+    stays = lax.div(b, 8) == core
+    own_gated = pltpu.make_async_copy(gated_src.at[core, lax.rem(b, 8)], gate_out.at[b], gated_recv.at[b])
+    for q in range(1, 8):
+        gated_copy(q, 0).start()
+        gated_copy(q, 1).start()
+    gated_copy(0, 1).start()
+
+    @pl.when(stays)
+    def _():
+        own_gated.start()
+
+    @pl.when(jnp.logical_not(stays))
+    def _():
+        gated_copy(0, 0).start()
+
+    for p in ORDER:
+        gate_copy(p).wait()
+    own_gate.wait()
+    for p in ORDER:
+        for s in range(2):
+            g_copy(p, 0, s).wait()
+            g_copy(p, 1, s).wait()
+    for s in range(2):
+        g_copy(0, 1, s).wait()
+        own_g[s].wait()
+    g = jnp.concatenate([g_came[h, s].reshape(rows, 128) for h in range(2) for s in range(2)], axis=1)
     g = g.astype(f32)
-    def done_copy(n, p):
-        to = peer(p)
-        return remote(done.at[n, to], came.at[n, b], done_send.at[n, p], done_recv.at[n, p], to, k)
-
-    own_done = {}
-
-    def put(n, value):
-        done[n] = to_columns(value).astype(bf16).reshape(BLOCKS, HELD, ROWS)
-        for p in ORDER:
-            done_copy(n, p).start()
-        own_done[n] = bring(done.at[n, b], came.at[n, b])
-
-    put(0, g * with_skip)
-    dy = (g * early[:, 2].reshape(rows, ROWS).astype(f32)).astype(bf16)
+    dy = (g * gate_came[...].reshape(rows, ROWS).astype(f32)).astype(bf16)
     y_re, y_im = forward(dy, *forward_tables)
 
+    def done_copy(p):
+        to = peer(p)
+        return remote(done.at[to], came.at[b], done_send.at[p], done_recv.at[p], to, k)
+
     lag = inverse(y_re * x_re + y_im * x_im, y_im * x_re - y_re * x_im, *inverse_tables)
-    put(1, lag * (1.0 / math.sqrt(BLOCKS * ROWS)))
+    done[...] = to_columns(lag * (1.0 / math.sqrt(BLOCKS * ROWS))).astype(bf16).reshape(BLOCKS, HELD, ROWS)
+    for p in ORDER:
+        done_copy(p).start()
+    own_done = bring(done.at[b], came.at[b])
     grad = inverse(h_re * y_re + h_im * y_im, h_re * y_im - h_im * y_re, *inverse_tables)
     columns = to_columns(grad + skip * dy.astype(f32))
     for p in ORDER:
@@ -338,26 +407,40 @@
         box_copy(p).start()
     own_box = bring(outbox.at[b], rows_out.at[b])
 
-    def arrived(n):
-        for p in ORDER:
-            done_copy(n, p).wait()
-        own_done[n].wait()
-        return came[n].reshape(rows, ROWS)
-
-    results = []
-    for n, out in enumerate((gate_out, filter_out)):
-        turned[n] = arrived(n).T
-        results.append(bring(turned.at[n], out))
+    for p in ORDER:
+        done_copy(p).wait()
+    own_done.wait()
+    turned[...] = came[...].reshape(rows, ROWS).T
+    result = bring(turned, filter_out)
     for c in range(2):
         for way in range(2):
-            far_copy(way, c).wait_send()
             for part in range(2):
+                far_copy(way, c, part).wait_send()
                 side_copy(way, part, c).wait_send()
+
+    def gated_arrived(i):
+        return remote(gated_src.at[0, 0], gate_out.at[i], gated_send.at[0, 0], gated_recv.at[i], b, mate)
+
+    for p in ORDER:
+        gated_arrived(lax.rem(b + p, BLOCKS)).wait_recv()
+    for q in range(1, 8):
+        gated_copy(q, 0).wait_send()
+        gated_copy(q, 1).wait_send()
+    gated_copy(0, 1).wait_send()
+
+    @pl.when(stays)
+    def _():
+        own_gated.wait()
+
+    @pl.when(jnp.logical_not(stays))
+    def _():
+        gated_copy(0, 0).wait_send()
+        gated_arrived(b).wait_recv()
+
     for p in ORDER:
         box_copy(p).wait()
     own_box.wait()
-    for copy in results:
-        copy.wait()
+    result.wait()
 
 
 ORDER = sorted(range(1, BLOCKS), key=lambda p: -(min(p // 4, 4 - p // 4) + min(p % 4, 4 - p % 4)))
@@ -431,13 +514,13 @@
     f32, bf16 = jnp.float32, jnp.bfloat16
     constants = tables()
     operands = (
-        tokens_in, filters, gate, skip.reshape(1, channels), out_grad.reshape(2, 2, half // 2, ROWS), out_weight,
+        tokens_in, filters, gate, skip.reshape(1, channels), out_grad.reshape(2, 2, 2, 64, ROWS), out_weight,
         owner, slot, *constants,
     )
     gate_grad, filter_grad, grad_rows = pl.pallas_call(
         kernel,
         out_shape=(
-            jax.ShapeDtypeStruct((ROWS, channels), bf16),
+            jax.ShapeDtypeStruct((BLOCKS, ROWS // BLOCKS, channels), bf16),
             jax.ShapeDtypeStruct((ROWS, channels), bf16),
             jax.ShapeDtypeStruct((BLOCKS, HELD, BLOCKS * send_rows), bf16),
         ),
@@ -450,21 +533,27 @@
             pltpu.VMEM(slot.shape, jnp.int32),
             *(pltpu.VMEM(c.shape, c.dtype) for c in constants),
             pltpu.VMEM((2, channels, 8 * ROWS), bf16),
-            pltpu.VMEM((8, 2, half // 2, ROWS), bf16),
+            pltpu.VMEM((8, 2, 2, 64, ROWS), bf16),
             pltpu.VMEM((2 * channels, half), f32),
-            pltpu.VMEM((BLOCKS, 3, HELD, ROWS), bf16),
-            pltpu.VMEM((BLOCKS, 3, HELD, ROWS), bf16),
+            pltpu.VMEM((BLOCKS, 2, HELD, ROWS), bf16),
+            pltpu.VMEM((BLOCKS, 2, HELD, ROWS), bf16),
+            pltpu.VMEM((BLOCKS, HELD, ROWS), bf16),
+            pltpu.VMEM((BLOCKS, HELD, ROWS), bf16),
             pltpu.VMEM((2, BLOCKS, HELD, half), bf16),
             pltpu.VMEM((2, BLOCKS, HELD, half), bf16),
-            pltpu.VMEM((2, BLOCKS, HELD, ROWS), bf16),
-            pltpu.VMEM((2, BLOCKS, HELD, ROWS), bf16),
+            pltpu.VMEM((2, 2, BLOCKS, HELD, 128), bf16),
+            pltpu.VMEM((2, 2, BLOCKS, HELD, 128), bf16),
+            pltpu.VMEM((2, 8, ROWS // BLOCKS, channels), bf16),
+            pltpu.VMEM((BLOCKS, HELD, ROWS), bf16),
+            pltpu.VMEM((BLOCKS, HELD, ROWS), bf16),
             pltpu.VMEM((BLOCKS, HELD, BLOCKS * send_rows), bf16),
             pltpu.VMEM((8, 128), jnp.int32),
             pltpu.VMEM((BLOCKS, 8, 128), jnp.int32),
-            pltpu.VMEM((2, ROWS, channels), bf16),
-            dma((24,)), dma((2,)), dma((2,)), dma((2, 2, 2)), dma((2, 2, 2)), dma((2, 2)), dma((2, 2)),
-            dma((BLOCKS,)), dma((BLOCKS,)), dma((2, BLOCKS)), dma((2, BLOCKS)),
-            dma((2, BLOCKS)), dma((2, BLOCKS)), dma((BLOCKS,)), dma((BLOCKS,)), dma((BLOCKS,)), dma((BLOCKS,)),
+            pltpu.VMEM((ROWS, channels), bf16),
+            dma((24,)), dma((2,)), dma((2,)), dma((2, 2, 2)), dma((2, 2, 2)), dma((2, 2, 2)), dma((2, 2, 2)),
+            dma((BLOCKS,)), dma((BLOCKS,)), dma((BLOCKS,)), dma((BLOCKS,)), dma((2, BLOCKS)), dma((2, BLOCKS)),
+            dma((2, 2, BLOCKS)), dma((2, 2, BLOCKS)), dma((2, 8)), dma((BLOCKS,)),
+            dma((BLOCKS,)), dma((BLOCKS,)), dma((BLOCKS,)), dma((BLOCKS,)), dma((BLOCKS,)), dma((BLOCKS,)),
         ],
         compiler_params=pltpu.CompilerParams(
             collective_id=0, has_side_effects=True, vmem_limit_bytes=67043328
@@ -472,7 +561,7 @@
     )(*operands)
     gate_grad, filter_grad, grad_rows = finish(gate_grad, filter_grad, grad_rows.reshape(channels, -1))
     grid = (BLOCKS, ROWS // BLOCKS, channels)
-    return (gate_grad.reshape(grid), filter_grad.reshape(grid), grad_rows)
+    return (gate_grad, filter_grad.reshape(grid), grad_rows)
 
 
 def solution(mesh):

time: 54.9 us -> 55.7 us (1.015)
  Pallas kernels: 54.2 us -> 54.9 us
    pallas_call x1, Pallas kernels: 51.8 us -> 52.5 us  [shards(): pl.pallas_call(kernel, out_shape=(jax.ShapeDtypeStruct((BLOCKS, ROWS // B...]
where the time goes in v6:
time: 55.7 us; the launch traced here: 55.5 us
  Pallas kernels  54.9 us (99%)
  between operations  0.64 us (1%)
    pallas_call x1, Pallas kernels, shards(): pl.pallas_call(kernel, out_shape=(jax.ShapeDtypeStruct((BLOCKS, ROWS // B...  52.5 us
    pallas_call x1, Pallas kernels, finish(): pl.pallas_call(finish_kernel, out_shape=(jax.ShapeDtypeStruct(gate_grad.s...  2.38 us

profile of v6, /device:TPU:1, one launch (start us, length us, event | category | flops | bytes accessed | tf_op | source)
XLA Modules:
  0.0 55.5 jit_solution(1479584940598760558)
XLA Ops:
  0.6 52.5 %shard_map.157 = (bf16[16,32,256]{2,1,0:T(8,128)(2,1)}, bf16[512,256]{1,0:T(8,128)(2,1)}, bf16[16,16,1024]{2,1,0:T(8,128)(2,1)}) custom-call(bf16[512,256]{1,0:T(8,128)(2,1)} %x_hbm.1, bf16[512,256]{1,0:T(8,128)(2,1)} %h_hbm.1, bf16[512,256]{1,0:T(8,128)(2,1)} %gate_hbm.1, f32[1,256]{1,0:T(1,128)} %bitcast.6, bf16[2,2,2,64,512]{4,3,2,1,0:T(8,128)(2,1)} %bitcast.4, ...), custom_call_target="tpu_custom_call" | custom-call | tf_op jit(solution)/shard_map/pallas_call | solution.py:520
  53.2 2.4 %shard_map.158 = (bf16[16,32,256]{2,1,0:T(8,128)(2,1)}, f32[512,256]{1,0:T(8,128)}, bf16[1024,256]{1,0:T(8,128)(2,1)}) custom-call(bf16[16,32,256]{2,1,0:T(8,128)(2,1)} %get-tuple-element.9.gate_hbm, bf16[512,256]{1,0:T(8,128)(2,1)} %get-tuple-element.10.filter_hbm, bf16[256,1024]{1,0:T(8,128)(2,1)} %bitcast.5), custom_call_target="tpu_custom_call" | custom-call | tf_op jit(solution)/shard_map/pallas_call | solution.py:487

commit v7 on v6

--- a/solution.py
+++ b/solution.py
@@ -100,6 +100,10 @@
         device_id=(bins, chan),
         device_id_type=pl.DeviceIdType.MESH,
     )
+
+
+def drain(ref, sem):
+    pltpu.make_async_copy(ref, ref, sem).wait()
 
 
 def kernel(
@@ -133,10 +137,11 @@
 
     local = []
 
-    def bring(src, dst):
-        copy = pltpu.make_async_copy(src, dst, local_sem.at[len(local)])
+    def bring(src, dst, sem=None):
+        copy = pltpu.make_async_copy(src, dst, local_sem.at[len(local)] if sem is None else sem)
         copy.start()
-        local.append(copy)
+        if sem is None:
+            local.append(copy)
         return copy
 
     own_raw = [bring(ref, raw.at[n]) for n, ref in enumerate((x_hbm, h_hbm, gate_hbm))]
@@ -163,7 +168,7 @@
         to = (right, left)[way]
         return remote(
             og_hbm.at[c, :, part], og_all.at[k, :, part],
-            side_send.at[way, part, c], side_recv.at[way, part, core], b, 2 * to + c,
+            side_send, side_recv.at[way, part], b, 2 * to + c,
         )
 
     for turn in range(2):
@@ -181,40 +186,36 @@
 
     def pair_copy(p):
         to = peer(p)
-        return remote(pair_src.at[to], pair.at[b], pair_send.at[p], pair_recv.at[p], to, k)
+        return remote(pair_src.at[to], pair.at[b], pair_send, pair_recv, to, k)
 
     for p in ORDER:
         pair_copy(p).start()
-    own_pair = bring(pair_src.at[b], pair.at[b])
+    bring(pair_src.at[b], pair.at[b], pair_recv)
     own_raw[2].wait()
     gate_src[...] = raw[2].T.reshape(BLOCKS, HELD, ROWS)
 
     def gate_copy(p):
         to = peer(p)
-        return remote(gate_src.at[to], gate_came.at[b], gate_send.at[p], gate_recv.at[p], to, k)
+        return remote(gate_src.at[to], gate_came.at[b], gate_send, gate_recv, to, k)
 
     for p in ORDER:
         gate_copy(p).start()
-    own_gate = bring(gate_src.at[b], gate_came.at[b])
-
-    def side_arrived(way, part, c):
-        src = 2 * (left, right)[way] + c
-        return remote(
-            og_hbm.at[c, :, part], og_all.at[src, :, part],
-            side_send.at[way, part, c], side_recv.at[way, part, c], b, mate,
-        )
+    bring(gate_src.at[b], gate_came.at[b], gate_recv)
+
+    def side_arrived(way, part):
+        src = 2 * (left, right)[way]
+        drain(og_all.at[pl.ds(src, 2), :, part], side_recv.at[way, part])
 
     def far_copy(way, c, s):
         src = 2 * (left, right)[way] + c
         to = (right, left)[way]
         return remote(
             og_all.at[src, s, way], og_all.at[src, s, way],
-            far_send.at[way, c, s], far_recv.at[way, c, s], b, 2 * to + core,
+            far_send, far_recv.at[s], b, 2 * to + core,
         )
 
-    for c in range(2):
-        for way in range(2):
-            side_arrived(way, way, c).wait_recv()
+    for way in range(2):
+        side_arrived(way, way)
     for s in range(2):
         for c in range(2):
             for way in range(2):
@@ -242,29 +243,27 @@
     lanes = lax.broadcasted_iota(jnp.int32, (rows, rows), 1)
     held = lax.rem(lax.broadcasted_iota(jnp.int32, (rows, rows), 0), HELD)
     skip = jnp.sum(jnp.where(lanes == held + HELD * b, skip_ref[...], 0.0), axis=1, keepdims=True)
-    for p in ORDER:
-        pair_copy(p).wait()
-    own_pair.wait()
+    drain(pair, pair_recv)
     x = pair[:, 0].reshape(rows, ROWS)
     x_re, x_im = forward(x, *forward_tables)
     h_re, h_im = forward(pair[:, 1].reshape(rows, ROWS), *forward_tables)
     conv = inverse(x_re * h_re - x_im * h_im, x_re * h_im + x_im * h_re, *inverse_tables)
     with_skip = (conv + skip * x.astype(f32)).astype(bf16)
     for hand in range(2):
-        mix_src[hand] = with_skip[:, rows * hand : rows * (hand + 1)].reshape(BLOCKS, HELD, ROWS // 2)
+        mix_src[BLOCKS * hand : BLOCKS * (hand + 1)] = with_skip[:, rows * hand : rows * (hand + 1)].reshape(BLOCKS, HELD, ROWS // 2)
 
     def mix_copy(p, c):
         to = peer(p)
         hand = lax.rem(core + c, 2)
         return remote(
-            mix_src.at[hand, to], mix.at[core, b], mix_send.at[c, p], mix_recv.at[c, p], to, 2 * chip + hand
+            mix_src.at[BLOCKS * hand + to], mix.at[core, b], mix_send, mix_recv, to, 2 * chip + hand
         )
 
     for p in ORDER:
         mix_copy(p, 0).start()
         mix_copy(p, 1).start()
     mix_copy(0, 1).start()
-    own_mix = bring(mix_src.at[core, b], mix.at[core, b])
+    bring(mix_src.at[BLOCKS * core + b], mix.at[core, b], mix_recv)
 
     odd = lax.rem(b, 2)
     target = (owner_ref[...] + odd * (1 - 2 * lax.rem(owner_ref[...], 2))) * send_rows + slot_ref[...] - b * send_rows
@@ -282,60 +281,52 @@
 
     def map_copy(p):
         to = peer(p)
-        return remote(map_src, maps.at[b], map_send.at[p], map_recv.at[p], to, k)
+        return remote(map_src, maps.at[b], map_send, map_recv, to, k)
 
     for p in ORDER:
         map_copy(p).start()
-    own_map = bring(map_src, maps.at[b])
-
-    for c in range(2):
-        for way in range(2):
-            side_arrived(way, 1 - way, c).wait_recv()
+    bring(map_src, maps.at[b], map_recv)
+
+    for way in range(2):
+        side_arrived(way, 1 - way)
+        for c in range(2):
             acc[...] += near(2 * (left, right)[way] + c)
 
     def g_copy(p, c, s):
         to = peer(p)
         hand = lax.rem(core + c, 2)
         return remote(
-            g_src.at[s, hand, to], g_came.at[core, s, b],
-            g_send.at[s, c, p], g_recv.at[s, c, p], to, 2 * chip + hand,
+            g_src.at[s, BLOCKS * hand + to], g_came.at[s, core, b], g_send.at[s], g_recv.at[s], to, 2 * chip + hand
         )
 
-    own_g = []
     for s in range(2):
-        for c in range(2):
-            for way in range(2):
-                far_copy(way, c, s).wait_recv()
+        drain(og_all.at[pl.ds(2 * across, 2), s], far_recv.at[s])
         part = acc[:, 128 * s : 128 * (s + 1)]
         for c in range(2):
             part = part + term(2 * across + c, og_all[2 * across + c, s].reshape(128, ROWS))
-        g_src[s] = part.astype(bf16).reshape(2, BLOCKS, HELD, 128)
+        g_src[s] = part.astype(bf16).reshape(2 * BLOCKS, HELD, 128)
         for p in ORDER:
             g_copy(p, 0, s).start()
             g_copy(p, 1, s).start()
         g_copy(0, 1, s).start()
-        own_g.append(bring(g_src.at[s, core, b], g_came.at[core, s, b]))
-
-    for p in ORDER:
-        mix_copy(p, 0).wait()
-        mix_copy(p, 1).wait()
-    mix_copy(0, 1).wait()
-    own_mix.wait()
+        bring(g_src.at[s, BLOCKS * core + b], g_came.at[s, core, b], g_recv.at[s])
+
+    drain(mix, mix_recv)
     g_block = jnp.concatenate([g_src[s].reshape(2 * rows, 128) for s in range(2)], axis=1).astype(f32)
     gated = (g_block * mix[...].reshape(2 * rows, ROWS // 2).astype(f32)).astype(bf16).T
     for hand in range(2):
-        gated_src[hand] = gated[:, rows * hand : rows * (hand + 1)].reshape(8, ROWS // BLOCKS, rows)
+        gated_src[8 * hand : 8 * (hand + 1)] = gated[:, rows * hand : rows * (hand + 1)].reshape(8, ROWS // BLOCKS, rows)
 
     def gated_copy(q, c):
         column = lax.rem(b + q, 8)
         hand = lax.rem(core + c, 2)
         return remote(
-            gated_src.at[hand, column], gate_out.at[b],
-            gated_send.at[c, q], gated_recv.at[b], 8 * core + column, 2 * chip + hand,
+            gated_src.at[8 * hand + column], gate_out.at[b],
+            gated_send, gated_recv, 8 * core + column, 2 * chip + hand,
         )
 
     stays = lax.div(b, 8) == core
-    own_gated = pltpu.make_async_copy(gated_src.at[core, lax.rem(b, 8)], gate_out.at[b], gated_recv.at[b])
+    own_gated = pltpu.make_async_copy(gated_src.at[8 * core + lax.rem(b, 8)], gate_out.at[b], gated_recv)
     for q in range(1, 8):
         gated_copy(q, 0).start()
         gated_copy(q, 1).start()
@@ -349,35 +340,26 @@
     def _():
         gated_copy(0, 0).start()
 
-    for p in ORDER:
-        gate_copy(p).wait()
-    own_gate.wait()
-    for p in ORDER:
-        for s in range(2):
-            g_copy(p, 0, s).wait()
-            g_copy(p, 1, s).wait()
+    drain(gate_came, gate_recv)
     for s in range(2):
-        g_copy(0, 1, s).wait()
-        own_g[s].wait()
-    g = jnp.concatenate([g_came[h, s].reshape(rows, 128) for h in range(2) for s in range(2)], axis=1)
+        drain(g_came.at[s], g_recv.at[s])
+    g = jnp.concatenate([g_came[s, h].reshape(rows, 128) for h in range(2) for s in range(2)], axis=1)
     g = g.astype(f32)
     dy = (g * gate_came[...].reshape(rows, ROWS).astype(f32)).astype(bf16)
     y_re, y_im = forward(dy, *forward_tables)
 
     def done_copy(p):
         to = peer(p)
-        return remote(done.at[to], came.at[b], done_send.at[p], done_recv.at[p], to, k)
+        return remote(done.at[to], came.at[b], done_send, done_recv, to, k)
 
     lag = inverse(y_re * x_re + y_im * x_im, y_im * x_re - y_re * x_im, *inverse_tables)
     done[...] = to_columns(lag * (1.0 / math.sqrt(BLOCKS * ROWS))).astype(bf16).reshape(BLOCKS, HELD, ROWS)
     for p in ORDER:
         done_copy(p).start()
-    own_done = bring(done.at[b], came.at[b])
+    bring(done.at[b], came.at[b], done_recv)
     grad = inverse(h_re * y_re + h_im * y_im, h_re * y_im - h_im * y_re, *inverse_tables)
     columns = to_columns(grad + skip * dy.astype(f32))
-    for p in ORDER:
-        map_copy(p).wait()
-    own_map.wait()
+    drain(maps, map_recv)
     low_half = lax.broadcasted_iota(jnp.int32, (HELD, 128), 1) < 64
     for m in range(BLOCKS // 2):
         picked = []
@@ -401,45 +383,38 @@
 
     def box_copy(p):
         to = peer(p)
-        return remote(outbox.at[to], rows_out.at[b], box_send.at[p], box_recv.at[p], to, k)
+        return remote(outbox.at[to], rows_out.at[b], box_send, box_recv, to, k)
 
     for p in ORDER:
         box_copy(p).start()
-    own_box = bring(outbox.at[b], rows_out.at[b])
-
-    for p in ORDER:
-        done_copy(p).wait()
-    own_done.wait()
+    bring(outbox.at[b], rows_out.at[b], box_recv)
+
+    drain(came, done_recv)
     turned[...] = came[...].reshape(rows, ROWS).T
     result = bring(turned, filter_out)
-    for c in range(2):
-        for way in range(2):
-            for part in range(2):
-                far_copy(way, c, part).wait_send()
-                side_copy(way, part, c).wait_send()
-
-    def gated_arrived(i):
-        return remote(gated_src.at[0, 0], gate_out.at[i], gated_send.at[0, 0], gated_recv.at[i], b, mate)
-
-    for p in ORDER:
-        gated_arrived(lax.rem(b + p, BLOCKS)).wait_recv()
-    for q in range(1, 8):
-        gated_copy(q, 0).wait_send()
-        gated_copy(q, 1).wait_send()
-    gated_copy(0, 1).wait_send()
+    drain(og_all.at[0:2], far_send)
+    drain(og_all.at[0:4], side_send)
+
+    drain(gate_out, gated_recv)
 
     @pl.when(stays)
     def _():
-        own_gated.wait()
+        drain(gated_src.at[0:15], gated_send)
 
     @pl.when(jnp.logical_not(stays))
     def _():
-        gated_copy(0, 0).wait_send()
-        gated_arrived(b).wait_recv()
-
-    for p in ORDER:
-        box_copy(p).wait()
-    own_box.wait()
+        drain(gated_src, gated_send)
+
+    few = BLOCKS - 1
+    drain(pair_src.at[0:few], pair_send)
+    drain(gate_src.at[0:few], gate_send)
+    drain(mix_src.at[0 : BLOCKS + few], mix_send)
+    for s in range(2):
+        drain(g_src.at[s, 0 : BLOCKS + few], g_send.at[s])
+    drain(maps.at[0:few], map_send)
+    drain(done.at[0:few], done_send)
+    drain(outbox.at[0:few], box_send)
+    drain(rows_out, box_recv)
     result.wait()
 
 
@@ -451,34 +426,33 @@
     odd = lax.rem(lax.axis_index("bins"), 2)
     span = 256
     parts = rows_hbm.shape[1] // span
-    reads, writes = [], []
+    reads = []
 
     def read(src, held):
         reads.append(pltpu.make_async_copy(src, held, sem.at[len(reads)]))
         reads[-1].start()
         return reads[-1]
 
-    def write(held, dst):
-        writes.append(pltpu.make_async_copy(held, dst, sem.at[8 + len(writes)]))
-        writes[-1].start()
+    def write(held, dst, at):
+        pltpu.make_async_copy(held, dst, sem.at[at]).start()
 
     taps_in = read(filter_hbm, taps)
     rows_in = [read(rows_hbm.at[:, pl.ds(n * span, span)], moved.at[n]) for n in range(parts)]
     gate_in = read(gate_hbm, gate)
     taps_in.wait()
     wide[...] = taps[...].astype(jnp.float32)
-    write(wide, filter_out)
+    write(wide, filter_out, 6)
     for n in range(parts):
         rows_in[n].wait()
         ranked[n] = moved[n].T.reshape(span // 64, 64, 256)
         for q in range(span // 64):
             group = n * (span // 64) + q
             group = group + odd * (1 - 2 * (q % 2))
-            write(ranked.at[n, q], rows_out.at[pl.ds(group * 64, 64)])
+            write(ranked.at[n, q], rows_out.at[pl.ds(group * 64, 64)], 7)
     gate_in.wait()
-    write(gate, gate_out)
-    for copy in writes:
-        copy.wait()
+    write(gate, gate_out, 8)
+    for ref, at in ((wide, 6), (ranked, 7), (gate, 8)):
+        drain(ref, sem.at[at])
 
 
 def finish(gate_grad, filter_grad, grad_rows):
@@ -499,7 +473,7 @@
             pltpu.VMEM(filter_grad.shape, f32),
             pltpu.VMEM((count // 256, channels, 256), grad_rows.dtype),
             pltpu.VMEM((count // 256, 4, 64, channels), grad_rows.dtype),
-            pltpu.SemaphoreType.DMA((32,)),
+            pltpu.SemaphoreType.DMA((9,)),
         ],
         compiler_params=pltpu.CompilerParams(vmem_limit_bytes=67043328),
     )(gate_grad, filter_grad, grad_rows)
@@ -510,6 +484,7 @@
     send_rows = 2 * ROWS // BLOCKS
     half = ROWS // 2
     dma = pltpu.SemaphoreType.DMA
+    one = dma(())
     hbm = pl.BlockSpec(memory_space=pl.ANY)
     f32, bf16 = jnp.float32, jnp.bfloat16
     constants = tables()
@@ -539,21 +514,20 @@
             pltpu.VMEM((BLOCKS, 2, HELD, ROWS), bf16),
             pltpu.VMEM((BLOCKS, HELD, ROWS), bf16),
             pltpu.VMEM((BLOCKS, HELD, ROWS), bf16),
+            pltpu.VMEM((2 * BLOCKS, HELD, half), bf16),
             pltpu.VMEM((2, BLOCKS, HELD, half), bf16),
-            pltpu.VMEM((2, BLOCKS, HELD, half), bf16),
+            pltpu.VMEM((2, 2 * BLOCKS, HELD, 128), bf16),
             pltpu.VMEM((2, 2, BLOCKS, HELD, 128), bf16),
-            pltpu.VMEM((2, 2, BLOCKS, HELD, 128), bf16),
-            pltpu.VMEM((2, 8, ROWS // BLOCKS, channels), bf16),
+            pltpu.VMEM((16, ROWS // BLOCKS, channels), bf16),
             pltpu.VMEM((BLOCKS, HELD, ROWS), bf16),
             pltpu.VMEM((BLOCKS, HELD, ROWS), bf16),
             pltpu.VMEM((BLOCKS, HELD, BLOCKS * send_rows), bf16),
             pltpu.VMEM((8, 128), jnp.int32),
             pltpu.VMEM((BLOCKS, 8, 128), jnp.int32),
             pltpu.VMEM((ROWS, channels), bf16),
-            dma((24,)), dma((2,)), dma((2,)), dma((2, 2, 2)), dma((2, 2, 2)), dma((2, 2, 2)), dma((2, 2, 2)),
-            dma((BLOCKS,)), dma((BLOCKS,)), dma((BLOCKS,)), dma((BLOCKS,)), dma((2, BLOCKS)), dma((2, BLOCKS)),
-            dma((2, 2, BLOCKS)), dma((2, 2, BLOCKS)), dma((2, 8)), dma((BLOCKS,)),
-            dma((BLOCKS,)), dma((BLOCKS,)), dma((BLOCKS,)), dma((BLOCKS,)), dma((BLOCKS,)), dma((BLOCKS,)),
+            dma((15,)), dma((2,)), dma((2,)), one, dma((2, 2)), one, dma((2,)),
+            one, one, one, one, one, one, dma((2,)), dma((2,)), one, one,
+            one, one, one, one, one, one,
         ],
         compiler_params=pltpu.CompilerParams(
             collective_id=0, has_side_effects=True, vmem_limit_bytes=67043328

time: 55.7 us -> 51.8 us (0.930)
  Pallas kernels: 54.9 us -> 51 us
    pallas_call x1, Pallas kernels: 52.5 us -> 48.9 us  [shards(): pl.pallas_call(kernel, out_shape=(jax.ShapeDtypeStruct((BLOCKS, ROWS // B...]
where the time goes in v7:
time: 51.8 us; the launch traced here: 51.7 us
  Pallas kernels  51 us (98%)
  between operations  0.64 us (1%)
    pallas_call x1, Pallas kernels, shards(): pl.pallas_call(kernel, out_shape=(jax.ShapeDtypeStruct((BLOCKS, ROWS // B...  48.9 us
    pallas_call x1, Pallas kernels, finish(): pl.pallas_call(finish_kernel, out_shape=(jax.ShapeDtypeStruct(gate_grad.s...  2.17 us

profile of v7, /device:TPU:1, one launch (start us, length us, event | category | flops | bytes accessed | tf_op | source)
XLA Modules:
  0.0 51.7 jit_solution(8335496530607587615)
XLA Ops:
  0.6 48.9 %shard_map.157 = (bf16[16,32,256]{2,1,0:T(8,128)(2,1)}, bf16[512,256]{1,0:T(8,128)(2,1)}, bf16[16,16,1024]{2,1,0:T(8,128)(2,1)}) custom-call(bf16[512,256]{1,0:T(8,128)(2,1)} %x_hbm.1, bf16[512,256]{1,0:T(8,128)(2,1)} %h_hbm.1, bf16[512,256]{1,0:T(8,128)(2,1)} %gate_hbm.1, f32[1,256]{1,0:T(1,128)} %bitcast.6, bf16[2,2,2,64,512]{4,3,2,1,0:T(8,128)(2,1)} %bitcast.4, ...), custom_call_target="tpu_custom_call" | custom-call | tf_op jit(solution)/shard_map/pallas_call | solution.py:495
  49.5 2.2 %shard_map.158 = (bf16[16,32,256]{2,1,0:T(8,128)(2,1)}, f32[512,256]{1,0:T(8,128)}, bf16[1024,256]{1,0:T(8,128)(2,1)}) custom-call(bf16[16,32,256]{2,1,0:T(8,128)(2,1)} %get-tuple-element.9.gate_hbm, bf16[512,256]{1,0:T(8,128)(2,1)} %get-tuple-element.10.filter_hbm, bf16[256,1024]{1,0:T(8,128)(2,1)} %bitcast.5), custom_call_target="tpu_custom_call" | custom-call | tf_op jit(solution)/shard_map/pallas_call | solution.py:461

commit v8 on v7

--- a/solution.py
+++ b/solution.py
@@ -132,8 +132,24 @@
     right, left, across = lax.rem(chip + 1, 4), lax.rem(chip + 3, 4), lax.rem(chip + 2, 4)
     mate = 2 * chip + 1 - core
 
+    along_y = [4 * lax.rem(b_y + n, 4) for n in range(4)]
+    along_z = [lax.rem(b_z + n, 4) for n in range(4)]
+
     def peer(p):
-        return 4 * lax.rem(b_y + p // 4, 4) + lax.rem(b_z + p % 4, 4)
+        return along_y[p // 4] + along_z[p % 4]
+
+    barrier = pltpu.get_barrier_semaphore()
+
+    def greet(bins, chan):
+        pl.semaphore_signal(barrier, inc=1, device_id=(bins, chan), device_id_type=pl.DeviceIdType.MESH)
+
+    for p in ORDER:
+        greet(peer(p), k)
+        greet(peer(p), mate)
+    greet(b, mate)
+    for side in (right, left):
+        for c in range(2):
+            greet(b, 2 * side + c)
 
     local = []
 
@@ -150,18 +166,6 @@
     own_small = [bring(*pair) for pair in ((skip_hbm, skip_ref), (owner_hbm, owner_ref), (slot_hbm, slot_ref))]
     own_tables = [bring(*pair) for pair in zip(tables_hbm, tables_ref)]
 
-    barrier = pltpu.get_barrier_semaphore()
-
-    def greet(bins, chan):
-        pl.semaphore_signal(barrier, inc=1, device_id=(bins, chan), device_id_type=pl.DeviceIdType.MESH)
-
-    for p in ORDER:
-        greet(peer(p), k)
-        greet(peer(p), mate)
-    greet(b, mate)
-    for side in (right, left):
-        for c in range(2):
-            greet(b, 2 * side + c)
     pl.semaphore_wait(barrier, 2 * BLOCKS - 1 + 4)
 
     def side_copy(way, part, c):
@@ -211,7 +215,7 @@
         to = (right, left)[way]
         return remote(
             og_all.at[src, s, way], og_all.at[src, s, way],
-            far_send, far_recv.at[s], b, 2 * to + core,
+            far_send, far_recv.at[s, c], b, 2 * to + core,
         )
 
     for way in range(2):
@@ -300,9 +304,9 @@
         )
 
     for s in range(2):
-        drain(og_all.at[pl.ds(2 * across, 2), s], far_recv.at[s])
         part = acc[:, 128 * s : 128 * (s + 1)]
         for c in range(2):
+            drain(og_all.at[2 * across + c, s], far_recv.at[s, c])
             part = part + term(2 * across + c, og_all[2 * across + c, s].reshape(128, ROWS))
         g_src[s] = part.astype(bf16).reshape(2 * BLOCKS, HELD, 128)
         for p in ORDER:
@@ -329,8 +333,6 @@
     own_gated = pltpu.make_async_copy(gated_src.at[8 * core + lax.rem(b, 8)], gate_out.at[b], gated_recv)
     for q in range(1, 8):
         gated_copy(q, 0).start()
-        gated_copy(q, 1).start()
-    gated_copy(0, 1).start()
 
     @pl.when(stays)
     def _():
@@ -343,6 +345,8 @@
     drain(gate_came, gate_recv)
     for s in range(2):
         drain(g_came.at[s], g_recv.at[s])
+    for q in range(8):
+        gated_copy(q, 1).start()
     g = jnp.concatenate([g_came[s, h].reshape(rows, 128) for h in range(2) for s in range(2)], axis=1)
     g = g.astype(f32)
     dy = (g * gate_came[...].reshape(rows, ROWS).astype(f32)).astype(bf16)
@@ -525,7 +529,7 @@
             pltpu.VMEM((8, 128), jnp.int32),
             pltpu.VMEM((BLOCKS, 8, 128), jnp.int32),
             pltpu.VMEM((ROWS, channels), bf16),
-            dma((15,)), dma((2,)), dma((2,)), one, dma((2, 2)), one, dma((2,)),
+            dma((15,)), dma((2,)), dma((2,)), one, dma((2, 2)), one, dma((2, 2)),
             one, one, one, one, one, one, dma((2,)), dma((2,)), one, one,
             one, one, one, one, one, one,
         ],

time: 51.8 us -> 51.2 us (0.988)
    pallas_call x1, Pallas kernels: 48.9 us -> 48.3 us  [shards(): pl.pallas_call(kernel, out_shape=(jax.ShapeDtypeStruct((BLOCKS, ROWS // B...]
where the time goes in v8:
time: 51.2 us; the launch traced here: 51.1 us
  Pallas kernels  50.5 us (99%)
  between operations  0.64 us (1%)
    pallas_call x1, Pallas kernels, shards(): pl.pallas_call(kernel, out_shape=(jax.ShapeDtypeStruct((BLOCKS, ROWS // B...  48.3 us
    pallas_call x1, Pallas kernels, finish(): pl.pallas_call(finish_kernel, out_shape=(jax.ShapeDtypeStruct(gate_grad.s...  2.17 us

profile of v8, /device:TPU:1, one launch (start us, length us, event | category | flops | bytes accessed | tf_op | source)
XLA Modules:
  0.0 51.1 jit_solution(11375528650111279341)
XLA Ops:
  0.6 48.3 %shard_map.157 = (bf16[16,32,256]{2,1,0:T(8,128)(2,1)}, bf16[512,256]{1,0:T(8,128)(2,1)}, bf16[16,16,1024]{2,1,0:T(8,128)(2,1)}) custom-call(bf16[512,256]{1,0:T(8,128)(2,1)} %x_hbm.1, bf16[512,256]{1,0:T(8,128)(2,1)} %h_hbm.1, bf16[512,256]{1,0:T(8,128)(2,1)} %gate_hbm.1, f32[1,256]{1,0:T(1,128)} %bitcast.6, bf16[2,2,2,64,512]{4,3,2,1,0:T(8,128)(2,1)} %bitcast.4, ...), custom_call_target="tpu_custom_call" | custom-call | tf_op jit(solution)/shard_map/pallas_call | solution.py:499
  48.9 2.2 %shard_map.158 = (bf16[16,32,256]{2,1,0:T(8,128)(2,1)}, f32[512,256]{1,0:T(8,128)}, bf16[1024,256]{1,0:T(8,128)(2,1)}) custom-call(bf16[16,32,256]{2,1,0:T(8,128)(2,1)} %get-tuple-element.9.gate_hbm, bf16[512,256]{1,0:T(8,128)(2,1)} %get-tuple-element.10.filter_hbm, bf16[256,1024]{1,0:T(8,128)(2,1)} %bitcast.5), custom_call_target="tpu_custom_call" | custom-call | tf_op jit(solution)/shard_map/pallas_call | solution.py:465

commit v9 on v8

--- a/solution.py
+++ b/solution.py
@@ -27,14 +27,18 @@
     back = np.concatenate([back_re, back_im], axis=1)
     r = np.arange(ROWS)
     twist = 2.0 * np.pi * np.outer(k1, r) / LENGTH
-    inner = 2.0 * np.pi * (np.outer(r, r) % ROWS) / ROWS
+    m = np.arange(ROWS // 2)
+    fold = 2.0 * np.pi * m[None, :] / ROWS
+    inner = 2.0 * np.pi * (np.outer(m, m) % (ROWS // 2)) / (ROWS // 2)
     return (
         jnp.asarray(ahead, jnp.bfloat16),
         jnp.asarray(back, jnp.bfloat16),
         jnp.asarray(np.cos(twist)[:, None, :], jnp.float32),
         jnp.asarray(np.sin(twist)[:, None, :], jnp.float32),
-        jnp.asarray(np.cos(inner), jnp.bfloat16),
-        jnp.asarray(np.sin(inner), jnp.bfloat16),
+        jnp.asarray(np.cos(fold), jnp.float32),
+        jnp.asarray(np.sin(fold), jnp.float32),
+        jnp.asarray(np.block([[np.cos(inner), -np.sin(inner)], [np.sin(inner), np.cos(inner)]]), jnp.bfloat16),
+        jnp.asarray(np.block([[np.cos(inner), np.sin(inner)], [-np.sin(inner), np.cos(inner)]]), jnp.bfloat16),
     )
 
 
@@ -50,22 +54,31 @@
     return value.reshape(HALF * HELD, ROWS)
 
 
-def forward(value, ahead, tw_cos, tw_sin, in_cos, in_sin):
+def forward(value, ahead, tw_cos, tw_sin, fold_cos, fold_sin, inner, inner_back):
     part = mm(ahead, value)
     n = HALF * HELD
+    half = ROWS // 2
     re, im = stage_rows(part[:n]), stage_rows(part[n:])
     z_re = flat(re * tw_cos + im * tw_sin)
     z_im = flat(im * tw_cos - re * tw_sin)
-    z = jnp.concatenate([z_re, z_im], axis=0).astype(jnp.bfloat16)
-    by_cos, by_sin = mm(z, in_cos), mm(z, in_sin)
-    return by_cos[:n] + by_sin[n:], by_cos[n:] - by_sin[:n]
-
-
-def inverse(s_re, s_im, back, tw_cos, tw_sin, in_cos, in_sin):
+    diff_re, diff_im = z_re[:, :half] - z_re[:, half:], z_im[:, :half] - z_im[:, half:]
+    even = jnp.concatenate([z_re[:, :half] + z_re[:, half:], z_im[:, :half] + z_im[:, half:]], axis=1)
+    odd = jnp.concatenate(
+        [diff_re * fold_cos + diff_im * fold_sin, diff_im * fold_cos - diff_re * fold_sin], axis=1
+    )
+    bins = mm(jnp.concatenate([even, odd], axis=0).astype(jnp.bfloat16), inner)
+    return bins[:, :half], bins[:, half:]
+
+
+def inverse(s_re, s_im, back, tw_cos, tw_sin, fold_cos, fold_sin, inner, inner_back):
     n = HALF * HELD
-    q = jnp.concatenate([s_re, s_im], axis=0).astype(jnp.bfloat16)
-    by_cos, by_sin = mm(q, in_cos), mm(q, in_sin)
-    re, im = stage_rows(by_cos[:n] - by_sin[n:]), stage_rows(by_cos[n:] + by_sin[:n])
+    half = ROWS // 2
+    q = mm(jnp.concatenate([s_re, s_im], axis=1).astype(jnp.bfloat16), inner_back)
+    re, im = q[:, :half], q[:, half:]
+    odd_re = re[n:] * fold_cos - im[n:] * fold_sin
+    odd_im = im[n:] * fold_cos + re[n:] * fold_sin
+    re = stage_rows(jnp.concatenate([re[:n] + odd_re, re[:n] - odd_re], axis=1))
+    im = stage_rows(jnp.concatenate([im[:n] + odd_im, im[:n] - odd_im], axis=1))
     t_re = flat(re * tw_cos - im * tw_sin)
     t_im = flat(im * tw_cos + re * tw_sin)[HELD : BLOCKS * HELD]
     t = jnp.concatenate([t_re, t_im], axis=0).astype(jnp.bfloat16)
@@ -241,9 +254,8 @@
 
     for copy in own_small + own_tables:
         copy.wait()
-    ahead, back, tw_cos, tw_sin, in_cos, in_sin = (ref[...] for ref in tables_ref)
-    forward_tables = (ahead, tw_cos, tw_sin, in_cos, in_sin)
-    inverse_tables = (back, tw_cos, tw_sin, in_cos, in_sin)
+    ahead, back, *shared = (ref[...] for ref in tables_ref)
+    forward_tables, inverse_tables = (ahead, *shared), (back, *shared)
     lanes = lax.broadcasted_iota(jnp.int32, (rows, rows), 1)
     held = lax.rem(lax.broadcasted_iota(jnp.int32, (rows, rows), 0), HELD)
     skip = jnp.sum(jnp.where(lanes == held + HELD * b, skip_ref[...], 0.0), axis=1, keepdims=True)
@@ -423,7 +435,7 @@
 
 
 ORDER = sorted(range(1, BLOCKS), key=lambda p: -(min(p // 4, 4 - p // 4) + min(p % 4, 4 - p % 4)))
-TABLES = 6
+TABLES = 8
 
 
 def finish_kernel(gate_hbm, filter_hbm, rows_hbm, gate_out, filter_out, rows_out, gate, taps, wide, moved, ranked, sem):
@@ -529,7 +541,7 @@
             pltpu.VMEM((8, 128), jnp.int32),
             pltpu.VMEM((BLOCKS, 8, 128), jnp.int32),
             pltpu.VMEM((ROWS, channels), bf16),
-            dma((15,)), dma((2,)), dma((2,)), one, dma((2, 2)), one, dma((2, 2)),
+            dma((17,)), dma((2,)), dma((2,)), one, dma((2, 2)), one, dma((2, 2)),
             one, one, one, one, one, one, dma((2,)), dma((2,)), one, one,
             one, one, one, one, one, one,
         ],

time: 51.2 us -> 50.8 us (level)
  no operation moved by 1% of the time
where the time goes in v9:
time: 50.8 us; the launch traced here: 50.7 us
  Pallas kernels  50 us (98%)
  between operations  0.64 us (1%)
    pallas_call x1, Pallas kernels, shards(): pl.pallas_call(kernel, out_shape=(jax.ShapeDtypeStruct((BLOCKS, ROWS // B...  47.9 us
    pallas_call x1, Pallas kernels, finish(): pl.pallas_call(finish_kernel, out_shape=(jax.ShapeDtypeStruct(gate_grad.s...  2.17 us

profile of v9, /device:TPU:1, one launch (start us, length us, event | category | flops | bytes accessed | tf_op | source)
XLA Modules:
  0.0 50.7 jit_solution(11926406702971561939)
XLA Ops:
  0.6 47.9 %shard_map.175 = (bf16[16,32,256]{2,1,0:T(8,128)(2,1)}, bf16[512,256]{1,0:T(8,128)(2,1)}, bf16[16,16,1024]{2,1,0:T(8,128)(2,1)}) custom-call(bf16[512,256]{1,0:T(8,128)(2,1)} %x_hbm.1, bf16[512,256]{1,0:T(8,128)(2,1)} %h_hbm.1, bf16[512,256]{1,0:T(8,128)(2,1)} %gate_hbm.1, f32[1,256]{1,0:T(1,128)} %bitcast.6, bf16[2,2,2,64,512]{4,3,2,1,0:T(8,128)(2,1)} %bitcast.4, ...), custom_call_target="tpu_custom_call" | custom-call | tf_op jit(solution)/shard_map/pallas_call | solution.py:511
  48.5 2.2 %shard_map.176 = (bf16[16,32,256]{2,1,0:T(8,128)(2,1)}, f32[512,256]{1,0:T(8,128)}, bf16[1024,256]{1,0:T(8,128)(2,1)}) custom-call(bf16[16,32,256]{2,1,0:T(8,128)(2,1)} %get-tuple-element.9.gate_hbm, bf16[512,256]{1,0:T(8,128)(2,1)} %get-tuple-element.10.filter_hbm, bf16[256,1024]{1,0:T(8,128)(2,1)} %bitcast.5), custom_call_target="tpu_custom_call" | custom-call | tf_op jit(solution)/shard_map/pallas_call | solution.py:477

commit v10 on v9

--- a/solution.py
+++ b/solution.py
@@ -54,20 +54,35 @@
     return value.reshape(HALF * HELD, ROWS)
 
 
-def forward(value, ahead, tw_cos, tw_sin, fold_cos, fold_sin, inner, inner_back):
+def chunk_of(value, s):
+    at, half = 128 * s, ROWS // 2
+    return jnp.concatenate([value[..., at : at + 128], value[..., half + at : half + at + 128]], axis=-1)
+
+
+def folded(value, s, ahead, tw_cos, tw_sin, fold_cos, fold_sin, inner, inner_back):
     part = mm(ahead, value)
     n = HALF * HELD
+    grid, plain = (HALF, HELD, 256), (n, 256)
+    re, im = part[:n].reshape(grid), part[n:].reshape(grid)
+    tw_cos, tw_sin = chunk_of(tw_cos, s), chunk_of(tw_sin, s)
+    z_re = (re * tw_cos + im * tw_sin).reshape(plain)
+    z_im = (im * tw_cos - re * tw_sin).reshape(plain)
+    fold_cos, fold_sin = fold_cos[:, 128 * s : 128 * (s + 1)], fold_sin[:, 128 * s : 128 * (s + 1)]
+    diff_re, diff_im = z_re[:, :128] - z_re[:, 128:], z_im[:, :128] - z_im[:, 128:]
+    re = jnp.concatenate([z_re[:, :128] + z_re[:, 128:], diff_re * fold_cos + diff_im * fold_sin], axis=0)
+    im = jnp.concatenate([z_im[:, :128] + z_im[:, 128:], diff_im * fold_cos - diff_re * fold_sin], axis=0)
+    return re.astype(jnp.bfloat16), im.astype(jnp.bfloat16)
+
+
+def binned(first, second, inner):
+    bins = mm(jnp.concatenate([first[0], second[0], first[1], second[1]], axis=1), inner)
     half = ROWS // 2
-    re, im = stage_rows(part[:n]), stage_rows(part[n:])
-    z_re = flat(re * tw_cos + im * tw_sin)
-    z_im = flat(im * tw_cos - re * tw_sin)
-    diff_re, diff_im = z_re[:, :half] - z_re[:, half:], z_im[:, :half] - z_im[:, half:]
-    even = jnp.concatenate([z_re[:, :half] + z_re[:, half:], z_im[:, :half] + z_im[:, half:]], axis=1)
-    odd = jnp.concatenate(
-        [diff_re * fold_cos + diff_im * fold_sin, diff_im * fold_cos - diff_re * fold_sin], axis=1
-    )
-    bins = mm(jnp.concatenate([even, odd], axis=0).astype(jnp.bfloat16), inner)
     return bins[:, :half], bins[:, half:]
+
+
+def forward(value, *forward_tables):
+    chunks = [folded(chunk_of(value, s), s, *forward_tables) for s in range(2)]
+    return binned(*chunks, forward_tables[-2])
 
 
 def inverse(s_re, s_im, back, tw_cos, tw_sin, fold_cos, fold_sin, inner, inner_back):
@@ -345,6 +360,8 @@
     own_gated = pltpu.make_async_copy(gated_src.at[8 * core + lax.rem(b, 8)], gate_out.at[b], gated_recv)
     for q in range(1, 8):
         gated_copy(q, 0).start()
+        gated_copy(q, 1).start()
+    gated_copy(0, 1).start()
 
     @pl.when(stays)
     def _():
@@ -355,14 +372,15 @@
         gated_copy(0, 0).start()
 
     drain(gate_came, gate_recv)
+    gate_rows = gate_came[...].reshape(rows, ROWS)
+    chunks, dys = [], []
     for s in range(2):
         drain(g_came.at[s], g_recv.at[s])
-    for q in range(8):
-        gated_copy(q, 1).start()
-    g = jnp.concatenate([g_came[s, h].reshape(rows, 128) for h in range(2) for s in range(2)], axis=1)
-    g = g.astype(f32)
-    dy = (g * gate_came[...].reshape(rows, ROWS).astype(f32)).astype(bf16)
-    y_re, y_im = forward(dy, *forward_tables)
+        g = jnp.concatenate([g_came[s, h].reshape(rows, 128) for h in range(2)], axis=1).astype(f32)
+        dys.append((g * chunk_of(gate_rows, s).astype(f32)).astype(bf16))
+        chunks.append(folded(dys[s], s, *forward_tables))
+    y_re, y_im = binned(*chunks, forward_tables[-2])
+    dy = jnp.concatenate([dys[s][:, 128 * h : 128 * (h + 1)] for h in range(2) for s in range(2)], axis=1)
 
     def done_copy(p):
         to = peer(p)

time: 50.8 us -> 50.7 us (level)
  no operation moved by 1% of the time
where the time goes in v10:
time: 50.7 us; the launch traced here: 50.6 us
  Pallas kernels  50 us (99%)
  between operations  0.64 us (1%)
    pallas_call x1, Pallas kernels, shards(): pl.pallas_call(kernel, out_shape=(jax.ShapeDtypeStruct((BLOCKS, ROWS // B...  47.8 us
    pallas_call x1, Pallas kernels, finish(): pl.pallas_call(finish_kernel, out_shape=(jax.ShapeDtypeStruct(gate_grad.s...  2.17 us

profile of v10, /device:TPU:1, one launch (start us, length us, event | category | flops | bytes accessed | tf_op | source)
XLA Modules:
  0.0 50.6 jit_solution(4456980635831362229)
XLA Ops:
  0.6 47.8 %shard_map.175 = (bf16[16,32,256]{2,1,0:T(8,128)(2,1)}, bf16[512,256]{1,0:T(8,128)(2,1)}, bf16[16,16,1024]{2,1,0:T(8,128)(2,1)}) custom-call(bf16[512,256]{1,0:T(8,128)(2,1)} %x_hbm.1, bf16[512,256]{1,0:T(8,128)(2,1)} %h_hbm.1, bf16[512,256]{1,0:T(8,128)(2,1)} %gate_hbm.1, f32[1,256]{1,0:T(1,128)} %bitcast.6, bf16[2,2,2,64,512]{4,3,2,1,0:T(8,128)(2,1)} %bitcast.4, ...), custom_call_target="tpu_custom_call" | custom-call | tf_op jit(solution)/shard_map/pallas_call | solution.py:529
  48.4 2.2 %shard_map.176 = (bf16[16,32,256]{2,1,0:T(8,128)(2,1)}, f32[512,256]{1,0:T(8,128)}, bf16[1024,256]{1,0:T(8,128)(2,1)}) custom-call(bf16[16,32,256]{2,1,0:T(8,128)(2,1)} %get-tuple-element.9.gate_hbm, bf16[512,256]{1,0:T(8,128)(2,1)} %get-tuple-element.10.filter_hbm, bf16[256,1024]{1,0:T(8,128)(2,1)} %bitcast.5), custom_call_target="tpu_custom_call" | custom-call | tf_op jit(solution)/shard_map/pallas_call | solution.py:495
